TPU v7x, 768 devices: a whole 4x8x12 slice. The times are simulated.
768 devices in a mesh: blk: 48 (over y, z_hi, core), col: 16 (over z_lo, x).
Axes of the slice: x: 4, y: 8, z: 12 (z_hi: 3, z_lo: 4; z = z_hi * 4 + z_lo), core: 2. Of those that a mesh axis runs over, the one named last changes fastest.
Arguments:
- features: bfloat16 [512, 196608], P('col', 'blk'), may hold values from -6 to 6
- band_weights: bfloat16 [196608, 384], P('blk'), may hold values from -0.3125 to 0.3125
- hub_ids: int32 [3072], P('blk'), may hold values from 0 to 196607, as said below
- tile_rows: int32 [6144], P('blk'), may hold values from 0 to 1535, as said below
- tile_cols: int32 [6144], P('blk'), may hold values from 0 to 23
- tile_vals: bfloat16 [6144, 128, 128], P('blk'), may hold values from -0.3125 to 0.3125
- tile_counts: int32 [48], P('blk'), may hold values from 1 to 128, as said below
- weight: bfloat16 [512, 512], replicated, may hold values from -0.25 to 0.25
- cotangent: bfloat16 [512, 196608], P('col', 'blk'), may hold values from -0.013671875 to 0.013671875
Outputs:
- activation: bfloat16 [512, 196608], P('col', 'blk')
- weight_grad: float32 [512, 512], P('col')
Inputs may be any that keep to these rules, and one draw needn't show every extreme that they name: `hub_ids`: each partition lists 64 distinct passages of its own rows, its first and its last passage among them. `tile_rows`: every slot of partition p names a row block of partition p's own passages; its slot 0 names the partition's first row block and its slot 1 its last. Partition p uses its first tile_counts[p] slots; some partition uses all 128.
All inputs are finite; a program needn't handle non-finite values.
Results may differ from a plain program's by a relative error of at most 0.0056.
Values may be sent and summed in bfloat16 or wider, within the bound.
A program may use at most 32 MiB of HBM per device.

v0:
```python
import jax
import jax.numpy as jnp
from jax import lax
from jax.sharding import PartitionSpec as P


def extended_2(x, sides, width):
    for axis, dim in sides:
        count, length = (lax.axis_size(axis), x.shape[dim])
        up = [(i, (i + 1) % count) for i in range(count)]
        down = [(j, i) for i, j in up]
        last = lax.slice_in_dim(x, length - width, length, axis=dim)
        leading = lax.slice_in_dim(x, 0, width, axis=dim)
        before = lax.ppermute(last, axis, up)
        after = lax.ppermute(leading, axis, down)
        x = jnp.concatenate([before, x, after], axis=dim)
    return x


def activate(preact, grad_in):
    activation = jax.nn.silu(preact).astype(jnp.bfloat16)
    sigmoid_pre = jax.nn.sigmoid(preact)
    pre_grad = (
        grad_in.astype(jnp.float32) * sigmoid_pre * (1.0 + preact * (1.0 - sigmoid_pre))
    ).astype(jnp.bfloat16)
    return (activation, pre_grad)


def outer_rows(left_side, right_side):
    return lax.dot_general(
        left_side, right_side, (((1,), (1,)), ((), ())), preferred_element_type=jnp.float32
    )


def body(
    features, band_weights, hub_ids, tile_rows, tile_cols, tile_vals, tile_counts, weight, cotangent
):
    feat_local, row_count = features.shape
    tile_size = tile_vals.shape[1]
    row_blocks = row_count // tile_size
    slot_count = tile_vals.shape[0]
    hidden_local = cotangent.shape[0]
    blk_index = lax.axis_index("blk")
    extended = extended_2(features, (("blk", 1),), tile_size)
    ext_blocks = extended.reshape(feat_local, row_blocks + 2, tile_size)
    windows = jnp.stack(
        [
            ext_blocks[:, 0:row_blocks],
            ext_blocks[:, 1 : row_blocks + 1],
            ext_blocks[:, 2 : row_blocks + 2],
        ],
        axis=2,
    )
    band_blocks = band_weights.reshape(row_blocks, tile_size, 3, tile_size)
    band_total = jnp.einsum(
        "fbsc,brsc->fbr", windows, band_blocks, preferred_element_type=jnp.float32
    )
    own_hubs = jnp.take(features, hub_ids - blk_index * row_count, axis=1)
    all_hubs = lax.all_gather(own_hubs, "blk", axis=1, tiled=True)
    hub_blocks = all_hubs.reshape(feat_local, all_hubs.shape[1] // tile_size, tile_size)
    sources = jnp.take(hub_blocks, tile_cols, axis=1)
    contrib = jnp.einsum("ftj,trj->ftr", sources, tile_vals, preferred_element_type=jnp.float32)
    in_use = (jnp.arange(slot_count) < tile_counts[0]).astype(jnp.float32)
    local_rows = tile_rows - blk_index * row_blocks
    hub_total = (
        jnp.zeros((feat_local, row_blocks, tile_size), jnp.float32)
        .at[:, local_rows, :]
        .add(contrib * in_use[None, :, None])
    )
    aggregated = (band_total + hub_total).reshape(feat_local, row_count).astype(jnp.bfloat16)
    gathered = lax.all_gather(aggregated, "col", axis=0, tiled=True)
    weight_rows = lax.dynamic_slice_in_dim(
        weight, lax.axis_index("col") * hidden_local, hidden_local, 0
    )
    preact = jnp.dot(weight_rows, gathered, preferred_element_type=jnp.float32)
    activation, pre_grad = activate(preact, cotangent)
    weight_grad = lax.psum(outer_rows(pre_grad, gathered), "blk")
    return (activation, weight_grad)


def solution(mesh):
    in_specs = (
        P("col", "blk"),
        P("blk", None),
        P("blk"),
        P("blk"),
        P("blk"),
        P("blk", None, None),
        P("blk"),
        P(),
        P("col", "blk"),
    )
    out_specs = (P("col", "blk"), P("col", None))
    return jax.shard_map(body, mesh=mesh, in_specs=in_specs, out_specs=out_specs, check_vma=False)
```

profile of v0, /device:TPU:1, one launch (start us, length us, event | category | flops | bytes accessed | tf_op | source)
XLA Modules:
  0.0 688.9 jit_solution(16504993884858160028)
XLA Ops:
  7.2 0.0 all-gather.3.cloned.1.call-start
  7.2 0.8 fusion.23
  8.0 12.0 %collective-permute-start = (bf16[32,128]{1,0:T(8,128)(2,1)S(1)}, bf16[32,128]{1,0:T(8,128)(2,1)S(1)}, u32[]{:S(2)}, u32[]{:S(2)}) collective-permute-start(bf16[32,128]{1,0:T(8,128)(2,1)S(1)} %get-tuple-element.7), channel_id=1, source_target_pairs={{0,16},{16,32},{32,48},{48,64},{64,80},{80,96},{96,112},{112,128},... | collective-permute-start | bytes 24584 | tf_op jit(solution)/shard_map/ppermute | solution.py:14
  20.0 2.3 collective-permute-start.1
  22.3 1.4 copy.45
  23.8 0.7 compare_and_fusion
  24.5 0.6 gather_fusion
  25.1 0.1 select_bitcast_fusion
  25.2 0.1 copy.46
  25.3 81.8 %all-gather = bf16[48,64,32]{1,2,0:T(8,128)(2,1)S(1)} all-gather(bf16[1,64,32]{1,2,0:T(8,128)(2,1)S(1)} %copy.46), channel_id=1, replica_groups=mesh['blk'=48,'col'=16] {'blk'}, dimensions={0}, use_global_device_ids=true | all-gather | bytes 200704 | tf_op jit(solution)/shard_map/all_gather | solution.py:59
  107.0 0.2 copy.47
  107.2 0.3 reshape.61
  107.5 0.7 compare_select_fusion.1
  108.8 0.7 compare_convert_fusion
  109.5 1.7 gather_fusion.1
  111.1 4.8 convolution_multiply_fusion
  116.0 9.0 %reshape.63 = bf16[32,128,3,128]{3,2,1,0:T(4,128)(2,1)} reshape(bf16[4096,384]{1,0:T(8,128)(2,1)} %param.10) | data formatting | bytes 6291456 | tf_op jit(solution)/shard_map/reshape | solution.py:54
  125.1 0.1 reshape.30
  125.2 0.2 fusion.22
  125.4 0.1 copy.67
  125.5 0.2 copy_bitcast_fusion.1
  125.7 3.4 fusion.2
  129.1 5.8 scatter_fusion
  134.9 0.7 copy_bitcast_fusion
  135.7 0.0 all-gather.3.cloned.1.call-update
  135.7 0.0 all-reduce.2.cloned.1.call-start
  135.7 77.9 %all-gather.3.cloned.1.call-done = bf16[512,4096]{1,0:T(8,128)(2,1)} async-done(((bf16[32,4096]{1,0:T(8,128)(2,1)}), bf16[512,4096]{1,0:T(8,128)(2,1)}) %all-gather.3.cloned.1.call-update) | async-done | bytes 4194320 | tf_op jit(solution)/shard_map/all_gather | solution.py:71
  213.6 3.9 multiply_convert_fusion.1
  217.5 2.0 fusion.14
  219.5 0.0 all-reduce.2.cloned.1.call-update
  219.5 461.1 %all-reduce.2.cloned.1.call-done = f32[32,512]{1,0:T(8,128)} async-done(((f32[32,512]{1,0:T(8,128)}), f32[32,512]{1,0:T(8,128)}) %all-reduce.2.cloned.1.call-update) | async-done | bytes 65552 | tf_op jit(solution)/shard_map/psum | solution.py:77
  680.6 1.5 copy.71
  (17 shorter events, 0.1 us)
Async XLA Ops:
  7.2 206.5 %copy-start = (bf16[512,512]{1,0:T(8,128)(2,1)S(1)}, bf16[512,512]{1,0:T(8,128)(2,1)}, u32[]{:S(2)}) copy-start(bf16[512,512]{1,0:T(8,128)(2,1)} %param.16) | copy-start | bytes 1572868
  7.2 206.4 %all-gather.3.cloned.1.call-start = ((), (), s32[]{:S(2)}) async-start(), calls=%async_computation | async-start | bytes 4456448 | tf_op jit(solution)/shard_map/all_gather | solution.py:71
  8.0 117.1 %collective-permute-start = (bf16[32,128]{1,0:T(8,128)(2,1)S(1)}, bf16[32,128]{1,0:T(8,128)(2,1)S(1)}, u32[]{:S(2)}, u32[]{:S(2)}) collective-permute-start(bf16[32,128]{1,0:T(8,128)(2,1)S(1)} %get-tuple-element.7), channel_id=1, source_target_pairs={{0,16},{16,32},{32,48},{48,64},{64,80},{80,96},{96,112},{112,128},... | collective-permute-start | bytes 24584 | tf_op jit(solution)/shard_map/ppermute | solution.py:14
  20.0 105.0 %collective-permute-start.1 = (bf16[32,128]{1,0:T(8,128)(2,1)S(1)}, bf16[32,128]{1,0:T(8,128)(2,1)S(1)}, u32[]{:S(2)}, u32[]{:S(2)}) collective-permute-start(bf16[32,128]{1,0:T(8,128)(2,1)S(1)} %get-tuple-element.8), channel_id=1, source_target_pairs={{16,0},{32,16},{48,32},{64,48},{80,64},{96,80},{112,96},{128,112},... | collective-permute-start | bytes 24584 | tf_op jit(solution)/shard_map/ppermute | solution.py:15
  111.1 4.8 copy-start.4
  116.0 9.1 %copy-start.2 = (bf16[32,4096]{1,0:T(8,128)(2,1)S(1)}, bf16[32,4096]{1,0:T(8,128)(2,1)}, u32[]{:S(2)}) copy-start(bf16[32,4096]{1,0:T(8,128)(2,1)} %param.9) | copy-start | bytes 786436
  134.9 82.6 %copy-start.3 = (bf16[32,4096]{1,0:T(8,128)(2,1)S(1)}, bf16[32,4096]{1,0:T(8,128)(2,1)}, u32[]{:S(2)}) copy-start(bf16[32,4096]{1,0:T(8,128)(2,1)} %param.17) | copy-start | bytes 786436
  135.7 544.9 %all-reduce.2.cloned.1.call-start = ((), (), s32[]{:S(2)}) async-start(), calls=%async_computation.1 | async-start | bytes 131072 | tf_op jit(solution)/shard_map/psum | solution.py:77
  213.6 3.9 copy-start.1
Sparse Core Ops, SparseCore 0:
  135.8 77.7 all-gather.2
  219.7 460.9 all-reduce.1
where the time goes:
time: 690 us; the launch traced here: 689 us
  waiting for transfers between devices  539 us (78%)
  blocking collectives  81.8 us (12%)
  local copies, waits for them, and re-layouts  16.2 us (2%)
  between operations  14.8 us (2%)
  starting transfers between devices  14.4 us (2%)
  matrix products  14.1 us (2%)
  other arithmetic  8.64 us (1%)
    psum x1, waiting for transfers between devices, body(): weight_grad = lax.psum(outer_rows(pre_grad, gathered), 'blk')  461 us
    all_gather x1, blocking collectives, body(): all_hubs = lax.all_gather(own_hubs, 'blk', axis=1, tiled=True)  81.8 us
    all_gather x1, waiting for transfers between devices, body(): gathered = lax.all_gather(aggregated, 'col', axis=0, tiled=True)  77.9 us
  transfers between devices with their start and end apart: 4, of which 2 were waited for; matrix products, arithmetic and copies ran while one was open for 3% of the time, Pallas kernels for 0%

commit v1 on v0

v1 whole, which is shorter than its diff:
```python
import functools

import jax
import jax.numpy as jnp
from jax import lax
from jax.experimental import pallas as pl
from jax.experimental.pallas import tpu as pltpu
from jax.sharding import PartitionSpec as P

MESH = pl.DeviceIdType.MESH
BF = jnp.bfloat16
F32 = jnp.float32
TILE = 128
NY, NZH, NC, NZL, NX = 8, 3, 2, 4, 4
CHIPS = NY * NZH
NZ = NZH * NZL
NYC = NY * NC
NT = (((1,), (1,)), ((), ()))
VMEM = pl.BlockSpec(memory_space=pltpu.VMEM)
ANY = pl.BlockSpec(memory_space=pl.ANY)
SMEM = pl.BlockSpec(memory_space=pltpu.SMEM)


def rcopy(src, dst, send, recv, blk, col):
    return pltpu.make_async_remote_copy(
        src_ref=src,
        dst_ref=dst,
        send_sem=send,
        recv_sem=recv,
        device_id={"blk": blk, "col": col},
        device_id_type=MESH,
    )


def signal(sem, blk, col):
    pl.semaphore_signal(sem, inc=1, device_id={"blk": blk, "col": col}, device_id_type=MESH)


def loop(start, stop, body):
    lax.fori_loop(start, stop, lambda i, c: (body(i), c)[1], 0)


def front_kernel(
    feat, bw, ids, cot, band, hubs, cotg, xe, wv, f_sem, w_sem, h_send, h_recv, s_sem, e_send, e_recv, c_send, c_recv, c_loc
):
    rows = bw.shape[0]
    blocks = rows // TILE
    quarter = rows // NZL
    wchunks = wv.shape[0]
    per = blocks // wchunks
    b = lax.axis_index("blk")
    c = lax.axis_index("col")
    core = lax.rem(b, NC)
    chip = lax.div(b, NC)
    z = lax.div(c, NX)
    x = lax.rem(c, NX)
    sib = b + 1 - 2 * core
    cross = lax.rem(b + 2 * core - 1 + CHIPS * NC, CHIPS * NC)

    f_copy = pltpu.make_async_copy(feat, xe.at[:, pl.ds(TILE, rows)], f_sem)
    f_copy.start()
    w_copies = [
        pltpu.make_async_copy(bw.at[pl.ds(i * per * TILE, per * TILE), :], wv.at[i], w_sem.at[i])
        for i in range(wchunks)
    ]
    for w in w_copies:
        w.start()

    barrier = pltpu.get_barrier_semaphore()

    def peer(d):
        return lax.rem(chip + d, CHIPS) * NC + core

    def zpeer(d):
        return lax.rem(z + d, NZL)

    loop(1, CHIPS, lambda d: signal(barrier, peer(d), c))
    signal(barrier, sib, c)
    signal(barrier, cross, c)
    for d in range(1, NZL):
        signal(barrier, b, zpeer(d) * NX + x)

    f_copy.wait()
    local_ids = ids[...] - b * rows
    lanes = jnp.concatenate([local_ids, local_ids], axis=1)
    step = 256
    picked = jnp.zeros((feat.shape[0], TILE), F32)
    for i in range(rows // step):
        at = lax.broadcasted_iota(jnp.int32, (step, TILE), 0) + i * step
        hot = jnp.where(at == lanes, 1.0, 0.0).astype(BF)
        picked += jnp.dot(xe[:, TILE + i * step : TILE + (i + 1) * step], hot, preferred_element_type=F32)
    half = feat.shape[0] // 2
    low = lax.broadcasted_iota(jnp.int32, (half, TILE), 1) < TILE // 2
    hubs[0, chip] = jnp.where(low, picked[:half], picked[half:]).astype(BF)

    pl.semaphore_wait(barrier, CHIPS - 1 + 2 + NZL - 1)

    def hub_copy(d):
        return rcopy(hubs.at[0, chip], hubs.at[0, chip], h_send.at[d], h_recv.at[d], peer(d), c)

    loop(1, CHIPS, lambda d: hub_copy(d).start())
    end = (blocks - 1) * TILE
    to_sib = rcopy(
        feat.at[:, pl.ds(pl.multiple_of((1 - core) * end, TILE), TILE)],
        xe.at[:, pl.ds(pl.multiple_of(core * (rows + TILE), TILE), TILE)],
        e_send.at[0], e_recv.at[0], sib, c,
    )
    to_cross = rcopy(
        feat.at[:, pl.ds(pl.multiple_of(core * end, TILE), TILE)],
        xe.at[:, pl.ds(pl.multiple_of((1 - core) * (rows + TILE), TILE), TILE)],
        e_send.at[1], e_recv.at[1], cross, c,
    )
    to_cross.start()
    to_sib.start()
    cots = []
    for d in range(1, NZL):
        zz = zpeer(d)
        cots.append(
            rcopy(
                cot.at[:, pl.ds(pl.multiple_of(zz * quarter, TILE), quarter)],
                cotg.at[z], c_send.at[d - 1], c_recv.at[d - 1], b, zz * NX + x,
            )
        )
    for k in cots:
        k.start()
    own_cot = pltpu.make_async_copy(
        cot.at[:, pl.ds(pl.multiple_of(z * quarter, TILE), quarter)], cotg.at[z], c_loc
    )
    own_cot.start()

    def do_band(r):
        i, j = divmod(r, per)
        band[r] = lax.dot_general(
            xe[:, r * TILE : (r + 3) * TILE],
            wv[i, j * TILE : (j + 1) * TILE, :],
            NT,
            preferred_element_type=F32,
        )

    for r in range(blocks):
        if r % per == 0:
            w_copies[r // per].wait()
        if 0 < r < blocks - 1:
            do_band(r)

    loop(1, CHIPS, lambda d: hub_copy(d).wait_recv())
    swap = rcopy(hubs.at[0], hubs.at[1], s_sem.at[0], s_sem.at[1], sib, c)
    swap.start()
    to_cross.wait_recv()
    to_sib.wait_recv()
    do_band(0)
    do_band(blocks - 1)
    swap.wait_recv()
    for k in cots:
        k.wait_recv()
    own_cot.wait()
    loop(1, CHIPS, lambda d: hub_copy(d).wait_send())
    swap.wait_send()
    to_cross.wait_send()
    to_sib.wait_send()
    for k in cots:
        k.wait_send()


def hub_kernel(rows_ref, cols_ref, count_ref, band, hubs, tv, out, tvv, hub, acc, t_sem):
    b = lax.axis_index("blk")
    core = lax.rem(b, NC)
    slots = tv.shape[0]
    blocks = band.shape[0]
    chunks = t_sem.shape[0]
    per = slots // chunks
    copies = [
        pltpu.make_async_copy(tv.at[pl.ds(i * per, per)], tvv.at[pl.ds(i * per, per)], t_sem.at[i])
        for i in range(chunks)
    ]
    for k in copies:
        k.start()
    acc[...] = band[...]
    half = hubs.shape[2]
    mine = hubs[0].astype(F32)
    other = hubs[1].astype(F32)
    first = jnp.where(core == 0, mine, other)
    second = jnp.where(core == 0, other, mine)
    low = lax.broadcasted_iota(jnp.int32, mine.shape, 2) < TILE // 2
    hub[:, :half, :] = jnp.where(low, first, pltpu.roll(second, TILE // 2, 2)).astype(BF)
    hub[:, half:, :] = jnp.where(low, pltpu.roll(first, TILE // 2, 2), second).astype(BF)
    count = count_ref[0]
    base = b * blocks
    for i in range(chunks):
        copies[i].wait()

        @pl.when(i * per < count)
        def _():
            parts = []
            for j in range(per):
                s = i * per + j
                got = lax.dot_general(hub[cols_ref[s]], tvv[s], NT, preferred_element_type=F32)
                parts.append(jnp.where(s < count, got, 0.0))
            for j in range(per):
                r = rows_ref[i * per + j] - base
                acc[r] = acc[r] + parts[j]

    for r in range(blocks):
        out[:, r * TILE : (r + 1) * TILE] = acc[r].astype(BF)


def back_kernel(
    agg, cotg, w3, act_out, wg_out, g, cotv, act, pt, yb, st, zb,
    z_send, z_recv, z_loc, x_send, x_recv, r_send, r_recv, cot_sem,
    a_send, a_recv, a_loc, y_send, y_recv, q_send, q_recv, o_send, o_recv,
):
    rows = agg.shape[1]
    feat_local = agg.shape[0]
    quarter = rows // NZL
    b = lax.axis_index("blk")
    c = lax.axis_index("col")
    core = lax.rem(b, NC)
    y = lax.div(b, NC * NZH)
    zh = lax.rem(lax.div(b, NC), NZH)
    z = lax.div(c, NX)
    x = lax.rem(c, NX)
    right = lax.rem(x + 1, NX)
    left = lax.rem(x + NX - 1, NX)
    me_yc = y * NC + core
    zz_me = zh * NZL + z

    def yc_blk(j):
        return (lax.div(j, NC) * NZH + zh) * NC + lax.rem(j, NC)

    def yc_peer(d):
        return lax.rem(me_yc + d, NYC)

    def z_peer(d):
        at = lax.rem(zz_me + d, NZ)
        return lax.div(at, NZL), lax.rem(at, NZL)

    def z_dev(d):
        h, l = z_peer(d)
        return (y * NZH + h) * NC + core, l * NX + x

    def zl(d):
        return lax.rem(z + d, NZL)

    ccopy = pltpu.make_async_copy(cotg, cotv, cot_sem)
    ccopy.start()
    barrier = pltpu.get_barrier_semaphore()
    for d in range(1, NZL):
        signal(barrier, b, zl(d) * NX + x)
    signal(barrier, b, z * NX + left)
    signal(barrier, b, z * NX + right)
    loop(1, NYC, lambda d: signal(barrier, yc_blk(yc_peer(d)), c))
    loop(1, NZ, lambda d: signal(barrier, *z_dev(d)))
    pl.semaphore_wait(barrier, NZL - 1 + 2 + NYC - 1 + NZ - 1)

    def part(ref, q):
        return ref.at[:, pl.ds(pl.multiple_of(q * quarter, TILE), quarter)]

    zc = [
        rcopy(part(agg, zl(d)), g.at[c], z_send.at[d - 1], z_recv.at[d - 1], b, zl(d) * NX + x)
        for d in range(1, NZL)
    ]
    for k in zc:
        k.start()
    own = pltpu.make_async_copy(part(agg, z), g.at[c], z_loc)
    own.start()

    def x_copy(src_z, src_x, to, send, recv):
        slot = src_z * NX + src_x
        return rcopy(g.at[slot], g.at[slot], send, recv, b, z * NX + to)

    def push(d):
        src = lax.rem(z + NZL - d, NZL)
        x_copy(src, x, right, x_send.at[0, src], x_recv.at[0, src]).start()
        x_copy(src, x, left, x_send.at[1, src], x_recv.at[1, src]).start()

    own.wait()
    push(0)
    for d in range(1, NZL):
        zc[d - 1].wait_recv()
        push(d)
    for s in range(NZL // 2):
        t = s + NZL // 2
        x_copy(s, left, right, x_send.at[0, s], x_recv.at[0, s]).wait_recv()
        x_copy(s, left, right, r_send.at[0, s], r_recv.at[0, s]).start()
        x_copy(t, right, left, x_send.at[1, t], x_recv.at[1, t]).wait_recv()
        x_copy(t, right, left, r_send.at[1, s], r_recv.at[1, s]).start()
    for s in range(NZL // 2):
        t = s + NZL // 2
        x_copy(t, left, right, x_send.at[0, t], x_recv.at[0, t]).wait_recv()
        x_copy(s, right, left, x_send.at[1, s], x_recv.at[1, s]).wait_recv()
    for s in range(NZL // 2):
        x_copy(s, left, right, r_send.at[0, s], r_recv.at[0, s]).wait_recv()
        x_copy(s, left, right, r_send.at[1, s], r_recv.at[1, s]).wait_recv()

    whole = g[...].reshape(NZL * NX * feat_local, quarter)
    ccopy.wait()
    pres = []
    for s in range(NZL):
        pre = jnp.dot(w3[s * NX + x], whole, preferred_element_type=F32)
        sig = jax.nn.sigmoid(pre)
        act[s] = (pre * sig).astype(BF)
        pres.append((cotv[s].astype(F32) * sig * (1.0 + pre * (1.0 - sig))).astype(BF))

    ac = [
        rcopy(act.at[zl(d)], part(act_out, z), a_send.at[d - 1], a_recv.at[d - 1], b, zl(d) * NX + x)
        for d in range(1, NZL)
    ]
    for k in ac:
        k.start()
    own_act = pltpu.make_async_copy(act.at[z], part(act_out, z), a_loc)
    own_act.start()

    for s in range(NZL):
        wg = lax.dot_general(pres[s], whole, NT, preferred_element_type=F32)
        for j in range(NYC):
            rt, lt = divmod(j, 4)
            pt[j, s] = wg[rt * 8 : (rt + 1) * 8, lt * TILE : (lt + 1) * TILE]

    def y_copy(d):
        j = yc_peer(d)
        return rcopy(pt.at[j], yb.at[d], y_send.at[d], y_recv.at[d], yc_blk(j), c)

    loop(1, NYC, lambda d: y_copy(d).start())
    loop(1, NYC, lambda d: y_copy(d).wait_recv())
    total = pt[me_yc]
    for d in range(1, NYC):
        total = total + yb[d]
    st[...] = total

    def q_copy(d):
        return rcopy(st.at[z_peer(d)[1]], zb.at[d], q_send.at[d], q_recv.at[d], *z_dev(d))

    loop(1, NZ, lambda d: q_copy(d).start())
    loop(1, NZ, lambda d: q_copy(d).wait_recv())
    tile = st[z]
    for d in range(1, NZ):
        tile = tile + zb[d]
    wg_out[me_yc] = tile

    def o_copy(d):
        return rcopy(wg_out.at[me_yc], wg_out.at[me_yc], o_send.at[d], o_recv.at[d], yc_blk(yc_peer(d)), c)

    loop(1, NYC, lambda d: o_copy(d).start())
    for k in ac:
        k.wait_recv()
    own_act.wait()
    loop(1, NYC, lambda d: o_copy(d).wait_recv())

    for k in zc:
        k.wait_send()
    for s in range(NZL):
        x_copy(s, x, right, x_send.at[0, s], x_recv.at[0, s]).wait_send()
        x_copy(s, x, left, x_send.at[1, s], x_recv.at[1, s]).wait_send()
    for s in range(NZL // 2):
        x_copy(s, left, right, r_send.at[0, s], r_recv.at[0, s]).wait_send()
        x_copy(s, left, left, r_send.at[1, s], r_recv.at[1, s]).wait_send()
    for k in ac:
        k.wait_send()
    loop(1, NYC, lambda d: y_copy(d).wait_send())
    loop(1, NZ, lambda d: q_copy(d).wait_send())
    loop(1, NYC, lambda d: o_copy(d).wait_send())


DMA = pltpu.SemaphoreType.DMA


def body(
    features, band_weights, hub_ids, tile_rows, tile_cols, tile_vals, tile_counts, weight, cotangent
):
    fl, rows = features.shape
    blocks = rows // TILE
    quarter = rows // NZL
    slots = tile_vals.shape[0]
    cols = NZL * NX
    wchunks = 8
    sds = jax.ShapeDtypeStruct
    band, hubs, cotg = pl.pallas_call(
        front_kernel,
        name="front",
        out_shape=(
            sds((blocks, fl, TILE), F32),
            sds((2, CHIPS, fl // 2, TILE), BF),
            sds((NZL, fl, quarter), BF),
        ),
        in_specs=[ANY, ANY, VMEM, ANY],
        out_specs=(VMEM, VMEM, ANY),
        scratch_shapes=[
            pltpu.VMEM((fl, rows + 2 * TILE), BF),
            pltpu.VMEM((wchunks, rows // wchunks, 3 * TILE), BF),
            DMA, DMA((wchunks,)), DMA((CHIPS,)), DMA((CHIPS,)), DMA((2,)),
            DMA((2,)), DMA((2,)), DMA((3,)), DMA((3,)), DMA,
        ],
        compiler_params=pltpu.CompilerParams(
            collective_id=0, has_side_effects=True, vmem_limit_bytes=24 << 20
        ),
    )(features, band_weights, hub_ids.reshape(1, -1), cotangent)

    agg = pl.pallas_call(
        hub_kernel,
        name="hub",
        out_shape=sds((fl, rows), BF),
        in_specs=[SMEM, SMEM, SMEM, VMEM, VMEM, ANY],
        out_specs=VMEM,
        scratch_shapes=[
            pltpu.VMEM(tile_vals.shape, BF),
            pltpu.VMEM((CHIPS, fl, TILE), BF),
            pltpu.VMEM((blocks, fl, TILE), F32),
            DMA((16,)),
        ],
        compiler_params=pltpu.CompilerParams(vmem_limit_bytes=24 << 20),
    )(tile_rows, tile_cols, tile_counts, band, hubs, tile_vals)

    act, wg = pl.pallas_call(
        back_kernel,
        name="back",
        out_shape=(sds((fl, rows), BF), sds((NYC, 8, TILE), F32)),
        in_specs=[ANY, ANY, VMEM],
        out_specs=(ANY, VMEM),
        scratch_shapes=[
            pltpu.VMEM((cols, fl, quarter), BF),
            pltpu.VMEM((NZL, fl, quarter), BF),
            pltpu.VMEM((NZL, fl, quarter), BF),
            pltpu.VMEM((NYC, NZL, 8, TILE), F32),
            pltpu.VMEM((NYC, NZL, 8, TILE), F32),
            pltpu.VMEM((NZL, 8, TILE), F32),
            pltpu.VMEM((NZ, 8, TILE), F32),
            DMA((3,)), DMA((3,)), DMA, DMA((2, NZL)), DMA((2, NZL)), DMA((2, 2)), DMA((2, 2)), DMA,
            DMA((3,)), DMA((3,)), DMA, DMA((NYC,)), DMA((NYC,)), DMA((NZ,)), DMA((NZ,)),
            DMA((NYC,)), DMA((NYC,)),
        ],
        compiler_params=pltpu.CompilerParams(
            collective_id=1, has_side_effects=True, vmem_limit_bytes=24 << 20
        ),
    )(agg, cotg, weight.reshape(cols, fl, weight.shape[1]))
    grad = wg.reshape(4, 4, 8, TILE).transpose(0, 2, 1, 3).reshape(fl, 4 * TILE)
    return act, grad


def solution(mesh):
    in_specs = (
        P("col", "blk"),
        P("blk", None),
        P("blk"),
        P("blk"),
        P("blk"),
        P("blk", None, None),
        P("blk"),
        P(),
        P("col", "blk"),
    )
    out_specs = (P("col", "blk"), P("col", None))
    return jax.shard_map(body, mesh=mesh, in_specs=in_specs, out_specs=out_specs, check_vma=False)
```

time: 690 us -> 91.7 us (0.13)
  waiting for transfers between devices: 539 us -> 0 us
  blocking collectives: 81.8 us -> 0 us
  Pallas kernels: 0 us -> 80.8 us
  starting transfers between devices: 14.4 us -> 0 us
  matrix products: 14.1 us -> 0 us
  between operations: 14.8 us -> 1.33 us
  other arithmetic: 8.64 us -> 0 us
  local copies, waits for them, and re-layouts: 16.2 us -> 9.27 us
    psum x1 -> x0, waiting for transfers between devices: 461 us -> none  [body(): weight_grad = lax.psum(outer_rows(pre_grad, gathered), 'blk')]
    all_gather x1 -> x0, blocking collectives: 81.8 us -> none  [body(): all_hubs = lax.all_gather(own_hubs, 'blk', axis=1, tiled=True)]
    pallas_call x0 -> x3, Pallas kernels: none -> 80.8 us  [the longest x1 47.1 us: body(): pl.pallas_call(back_kernel, name='back', out_shape=(sds((fl, rows), BF),...]
    all_gather x1 -> x0, waiting for transfers between devices: 77.9 us -> none  [body(): gathered = lax.all_gather(aggregated, 'col', axis=0, tiled=True)]
    ppermute x2 -> x0, starting transfers between devices: 14.3 us -> none  [the longest x1 12 us: extended_2(): before = lax.ppermute(last, axis, up)]
    dot_general x4 -> x0, matrix products: 14.1 us -> none  [the longest x1 4.84 us: body(): jnp.einsum('ftj,trj->ftr', sources, tile_vals, preferred_element_type=jnp...]
    reshape x3 -> x0, local copies, waits for them, and re-layouts: 9.21 us -> none  [the longest x1 9.02 us: body(): band_blocks = band_weights.reshape(row_blocks, tile_size, 3, tile_size)]
  transfers between devices with their start and end apart: 4 -> 0, of which waited for: 2 -> 0; matrix products, arithmetic and copies ran while one was open for 3% -> 0% of each run, Pallas kernels for 0% -> 0%
where the time goes in v1:
time: 91.7 us; the launch traced here: 91.4 us
  Pallas kernels  80.8 us (88%)
  local copies, waits for them, and re-layouts  9.27 us (10%)
  between operations  1.33 us (1%)
    pallas_call x1, Pallas kernels, body(): pl.pallas_call(back_kernel, name='back', out_shape=(sds((fl, rows), BF),...  47.1 us
    pallas_call x1, Pallas kernels, body(): pl.pallas_call(front_kernel, name='front', out_shape=(sds((blocks, fl, TI...  30.9 us
    unnamed x18, local copies, waits for them, and re-layouts  9.27 us
    pallas_call x1, Pallas kernels, body(): pl.pallas_call(hub_kernel, name='hub', out_shape=sds((fl, rows), BF), in_...  2.74 us

profile of v1, /device:TPU:1, one launch (start us, length us, event | category | flops | bytes accessed | tf_op | source)
XLA Modules:
  0.0 91.4 jit_solution(6120827113593946798)
XLA Ops:
  1.3 0.0 copy-start.1
  1.3 1.9 %copy-done.1 = bf16[4096,384]{1,0:T(8,128)(2,1)S(1)} copy-done((bf16[4096,384]{1,0:T(8,128)(2,1)S(1)}, bf16[4096,384]{1,0:T(8,128)(2,1)}, u32[]{:S(2)}) %copy-start.1) | copy-done | bytes 3145752
  3.2 0.0 copy-start.3
  3.2 0.9 %copy-done.3 = bf16[32,4096]{1,0:T(8,128)(2,1)S(1)} copy-done((bf16[32,4096]{1,0:T(8,128)(2,1)S(1)}, bf16[32,4096]{1,0:T(8,128)(2,1)}, u32[]{:S(2)}) %copy-start.3) | copy-done | bytes 262168
  4.1 0.0 copy-start.4
  4.1 0.9 %copy-done.4 = bf16[32,4096]{1,0:T(8,128)(2,1)S(1)} copy-done((bf16[32,4096]{1,0:T(8,128)(2,1)S(1)}, bf16[32,4096]{1,0:T(8,128)(2,1)}, u32[]{:S(2)}) %copy-start.4) | copy-done | bytes 262168
  5.1 0.0 copy-start.7
  5.1 0.7 copy-done.7
  5.7 0.0 copy-start.2
  5.7 30.9 %front.1 = (f32[32,32,128]{2,1,0:T(8,128)S(1)}, bf16[2,24,16,128]{3,2,1,0:T(8,128)(2,1)S(1)}, bf16[4,32,1024]{2,1,0:T(8,128)(2,1)S(1)}) custom-call(bf16[32,4096]{1,0:T(8,128)(2,1)S(1)} %copy-done.3, bf16[4096,384]{1,0:T(8,128)(2,1)S(1)} %copy-done.1, s32[1,64]{1,0:T(1,128)S(1)} %bitcast.9, bf16[32,4096]{1,0:T(8,128)(2,1)S(1)} %copy-done.4), custom_call_target="tpu_custom_call" | custom-call | tf_op jit(solution)/shard_map/front/pallas_call | solution.py:377
  36.7 0.0 copy-start
  36.7 2.2 %copy-done = bf16[128,128,128]{2,1,0:T(8,128)(2,1)S(1)} copy-done((bf16[128,128,128]{2,1,0:T(8,128)(2,1)S(1)}, bf16[128,128,128]{2,1,0:T(8,128)(2,1)}, u32[]{:S(2)}) %copy-start) | copy-done | bytes 4194328
  38.9 0.0 copy-start.5
  38.9 0.7 copy-done.5
  39.5 0.0 copy-start.6
  39.5 0.7 copy-done.6
  40.2 2.7 %hub.1.agg = bf16[32,4096]{1,0:T(8,128)(2,1)S(1)} custom-call(s32[128]{0:T(128)S(1)} %copy-done.5, s32[128]{0:T(128)S(1)} %copy-done.6, s32[1]{0:T(128)S(6)} %copy.13.count_ref, f32[32,32,128]{2,1,0:T(8,128)S(1)} %get-tuple-element.7.band, bf16[2,24,16,128]{3,2,1,0:T(8,128)(2,1)S(1)} %get-tuple-element.8.hubs, bf16[128,128,128]{2,1,0:T(8,128)(2,1)S(1)} %copy-done), custom_call_target="tpu_custom_call" | custom-call | tf_op jit(solution)/shard_map/hub/pallas_call | solution.py:398
  42.9 0.0 copy-done.2
  42.9 47.1 %back.1 = (bf16[32,4096]{1,0:T(8,128)(2,1)S(1)}, f32[16,8,128]{2,1,0:T(8,128)S(1)}) custom-call(bf16[32,4096]{1,0:T(8,128)(2,1)S(1)} %hub.1.agg, bf16[4,32,1024]{2,1,0:T(8,128)(2,1)S(1)} %get-tuple-element.9.cotg, bf16[16,32,512]{2,1,0:T(8,128)(2,1)S(1)} %bitcast.7), custom_call_target="tpu_custom_call" | custom-call | tf_op jit(solution)/shard_map/back/pallas_call | solution.py:413
  90.1 0.7 copy.14
  90.8 0.6 copy.15
Async XLA Ops:
  1.3 1.9 %copy-start.1 = (bf16[4096,384]{1,0:T(8,128)(2,1)S(1)}, bf16[4096,384]{1,0:T(8,128)(2,1)}, u32[]{:S(2)}) copy-start(bf16[4096,384]{1,0:T(8,128)(2,1)} %bw.1) | copy-start | bytes 9437188
  3.2 0.9 %copy-start.3 = (bf16[32,4096]{1,0:T(8,128)(2,1)S(1)}, bf16[32,4096]{1,0:T(8,128)(2,1)}, u32[]{:S(2)}) copy-start(bf16[32,4096]{1,0:T(8,128)(2,1)} %feat.1) | copy-start | bytes 786436
  4.1 0.9 %copy-start.4 = (bf16[32,4096]{1,0:T(8,128)(2,1)S(1)}, bf16[32,4096]{1,0:T(8,128)(2,1)}, u32[]{:S(2)}) copy-start(bf16[32,4096]{1,0:T(8,128)(2,1)} %cot.1) | copy-start | bytes 786436
  5.1 0.7 copy-start.7
  5.7 37.2 %copy-start.2 = (bf16[512,512]{1,0:T(8,128)(2,1)S(1)}, bf16[512,512]{1,0:T(8,128)(2,1)}, u32[]{:S(2)}) copy-start(bf16[512,512]{1,0:T(8,128)(2,1)} %param.16) | copy-start | bytes 1572868
  36.7 2.2 %copy-start = (bf16[128,128,128]{2,1,0:T(8,128)(2,1)S(1)}, bf16[128,128,128]{2,1,0:T(8,128)(2,1)}, u32[]{:S(2)}) copy-start(bf16[128,128,128]{2,1,0:T(8,128)(2,1)} %tv.1) | copy-start | bytes 12582916
  38.9 0.7 copy-start.5
  39.5 0.7 copy-start.6

commit v2 on v0

v2 whole, which is shorter than its diff:
```python
import functools

import jax
import jax.numpy as jnp
from jax import lax
from jax.experimental import pallas as pl
from jax.experimental.pallas import tpu as pltpu
from jax.sharding import PartitionSpec as P

MESH = pl.DeviceIdType.MESH
BF = jnp.bfloat16
F32 = jnp.float32
TILE = 128
NY, NZH, NC, NZL, NX = 8, 3, 2, 4, 4
CHIPS = NY * NZH
NZ = NZH * NZL
NT = (((1,), (1,)), ((), ()))
VMEM = pl.BlockSpec(memory_space=pltpu.VMEM)
ANY = pl.BlockSpec(memory_space=pl.ANY)
HBM = pl.BlockSpec(memory_space=pltpu.HBM)
SMEM = pl.BlockSpec(memory_space=pltpu.SMEM)


def rcopy(src, dst, send, recv, blk, col):
    return pltpu.make_async_remote_copy(
        src_ref=src,
        dst_ref=dst,
        send_sem=send,
        recv_sem=recv,
        device_id={"blk": blk, "col": col},
        device_id_type=MESH,
    )


def signal(sem, blk, col):
    pl.semaphore_signal(sem, inc=1, device_id={"blk": blk, "col": col}, device_id_type=MESH)


def loop(start, stop, body):
    lax.fori_loop(start, stop, lambda i, c: (body(i), c)[1], 0)


def layer_kernel(
    count, feat, bw, ids, row_ids, col_ids, tv, cot, w3, act_out, wg_out,
    xe, wv, idv, rowv, colv, tvv, cotg, w3v, band, hubs, hub, part_s, hub_sum, aggq, g, act, pres, pt, sb, qb, yb, st, zb,
    in_sem, h_send, h_recv, s_sem, e_send, e_recv, c_send, c_recv, c_loc,
    z_send, z_recv, z_loc, x_send, x_recv, r_send, r_recv, a_send, a_recv, a_loc,
    p_sem, y_send, y_recv, q_send, q_recv, o_send, o_recv, t_sem,
):
    rows = bw.shape[0]
    fl = feat.shape[0]
    blocks = rows // TILE
    quarter = rows // NZL
    per = quarter // TILE
    slots = tv.shape[0]
    b = lax.axis_index("blk")
    c = lax.axis_index("col")
    core = lax.rem(b, NC)
    chip = lax.div(b, NC)
    y = lax.div(chip, NZH)
    zh = lax.rem(chip, NZH)
    z = lax.div(c, NX)
    x = lax.rem(c, NX)
    sib = b + 1 - 2 * core
    cross = lax.rem(b + 2 * core - 1 + CHIPS * NC, CHIPS * NC)
    right = lax.rem(x + 1, NX)
    left = lax.rem(x + NX - 1, NX)
    zz_me = zh * NZL + z

    def hub_peer(d):
        return lax.rem(chip + d, CHIPS) * NC + core

    def zl(d):
        return lax.rem(z + d, NZL)

    def y_peer(d):
        return lax.rem(y + d, NY)

    def y_blk(at):
        return (at * NZH + zh) * NC + core

    def z_peer(d):
        at = lax.rem(zz_me + d, NZ)
        return lax.div(at, NZL), lax.rem(at, NZL)

    def z_dev(h, l):
        return (y * NZH + h) * NC + core, l * NX + x

    barrier = pltpu.get_barrier_semaphore()
    loop(1, CHIPS, lambda d: signal(barrier, hub_peer(d), c))
    signal(barrier, cross, c)
    for i in range(1, NZH):
        for d in range(1, NZL):
            signal(barrier, *z_dev(lax.rem(zh + i, NZH), zl(d)))
    for d in range(1, NZL):
        signal(barrier, b, zl(d) * NX + x)
    signal(barrier, b, z * NX + left)
    signal(barrier, b, z * NX + right)
    signal(barrier, sib, c)

    loads = [
        pltpu.make_async_copy(src, dst, in_sem.at[i])
        for i, (src, dst) in enumerate(
            [
                (feat, xe.at[:, pl.ds(TILE, rows)]),
                (ids, idv),
                (bw.at[pl.ds(0, rows // 2)], wv.at[pl.ds(0, rows // 2)]),
                (bw.at[pl.ds(rows // 2, rows // 2)], wv.at[pl.ds(rows // 2, rows // 2)]),
                (row_ids, rowv),
                (col_ids, colv),
                (tv, tvv),
                (w3, w3v),
            ]
        )
    ]
    for k in loads:
        k.start()

    loads[0].wait()
    loads[1].wait()
    local_ids = idv[...] - b * rows
    lanes = jnp.concatenate([local_ids, local_ids], axis=1)
    step = 256
    picked = jnp.zeros((fl, TILE), F32)
    for i in range(rows // step):
        at = lax.broadcasted_iota(jnp.int32, (step, TILE), 0) + i * step
        hot = jnp.where(at == lanes, 1.0, 0.0).astype(BF)
        picked += jnp.dot(xe[:, TILE + i * step : TILE + (i + 1) * step], hot, preferred_element_type=F32)
    half = fl // 2
    low = lax.broadcasted_iota(jnp.int32, (half, TILE), 1) < TILE // 2
    hubs[0, chip] = jnp.where(low, picked[:half], picked[half:]).astype(BF)

    pl.semaphore_wait(barrier, CHIPS - 1 + 1 + (NZH - 1) * (NZL - 1) + NZL - 1 + 2 + 1)

    def hub_copy(d):
        return rcopy(hubs.at[0, chip], hubs.at[0, chip], h_send.at[d], h_recv.at[d], hub_peer(d), c)

    loop(1, CHIPS, lambda d: hub_copy(d).start())
    end = (blocks - 1) * TILE
    to_sib = rcopy(
        feat.at[:, pl.ds(pl.multiple_of((1 - core) * end, TILE), TILE)],
        xe.at[:, pl.ds(pl.multiple_of(core * (rows + TILE), TILE), TILE)],
        e_send.at[0], e_recv.at[0], sib, c,
    )
    to_cross = rcopy(
        feat.at[:, pl.ds(pl.multiple_of(core * end, TILE), TILE)],
        xe.at[:, pl.ds(pl.multiple_of((1 - core) * (rows + TILE), TILE), TILE)],
        e_send.at[1], e_recv.at[1], cross, c,
    )
    to_cross.start()
    to_sib.start()

    def part(ref, q):
        return ref.at[:, pl.ds(pl.multiple_of(q * quarter, TILE), quarter)]

    cots = [
        rcopy(part(cot, zl(d)), cotg.at[z], c_send.at[d - 1], c_recv.at[d - 1], b, zl(d) * NX + x)
        for d in range(1, NZL)
    ]
    for k in cots:
        k.start()
    own_cot = pltpu.make_async_copy(part(cot, z), cotg.at[z], c_loc)
    own_cot.start()

    def do_band(r):
        band[r] = lax.dot_general(
            xe[:, r * TILE : (r + 3) * TILE], wv[r * TILE : (r + 1) * TILE, :], NT, preferred_element_type=F32
        )

    loads[2].wait()
    loads[3].wait()
    for r in range(1, blocks - 1):
        do_band(r)
    for k in loads[4:]:
        k.wait()
    same = lax.broadcasted_iota(jnp.int32, (blocks, slots), 0) == rowv[...] - b * blocks
    used = lax.broadcasted_iota(jnp.int32, (blocks, slots), 1) < count[0]
    place = jnp.where(same & used, 1.0, 0.0).astype(BF)
    place = jnp.concatenate([place, place], axis=1)

    loop(1, CHIPS, lambda d: hub_copy(d).wait_recv())
    swap = rcopy(hubs.at[0], hubs.at[1], s_sem.at[0], s_sem.at[1], sib, c)
    swap.start()
    to_cross.wait_recv()
    to_sib.wait_recv()
    do_band(0)
    do_band(blocks - 1)
    swap.wait_recv()

    mine = hubs[0].astype(F32)
    other = hubs[1].astype(F32)
    first = jnp.where(core == 0, mine, other)
    second = jnp.where(core == 0, other, mine)
    low3 = lax.broadcasted_iota(jnp.int32, mine.shape, 2) < TILE // 2
    hub[:, :half, :] = jnp.where(low3, first, pltpu.roll(second, TILE // 2, 2)).astype(BF)
    hub[:, half:, :] = jnp.where(low3, pltpu.roll(first, TILE // 2, 2), second).astype(BF)

    def some_slots(i):
        for j in range(8):
            s = i * 8 + j
            part_s[pl.ds(s, fl, stride=slots), :] = lax.dot_general(
                hub[colv[s]], tvv[s], NT, preferred_element_type=F32
            )

    loop(0, slots // 8, some_slots)
    for f in range(fl):
        value = part_s[f * slots : (f + 1) * slots, :]
        high = value.astype(BF)
        rest = (value - high.astype(F32)).astype(BF)
        hub_sum[pl.ds(f, blocks, stride=fl), :] = jnp.dot(
            place, jnp.concatenate([high, rest], axis=0), preferred_element_type=F32
        )

    def round_part(q):
        for j in range(per):
            r = q * per + j
            at = pl.ds(pl.multiple_of(r * fl, fl), fl)
            aggq[q, :, j * TILE : (j + 1) * TILE] = (band[r] + hub_sum[at, :]).astype(BF)

    zc = [
        rcopy(aggq.at[zl(d)], g.at[c], z_send.at[d - 1], z_recv.at[d - 1], b, zl(d) * NX + x)
        for d in range(1, NZL)
    ]
    for d in (2, 1, 3):
        round_part(zl(d))
        zc[d - 1].start()
    round_part(z)
    own = pltpu.make_async_copy(aggq.at[z], g.at[c], z_loc)
    own.start()

    def x_copy(src_z, src_x, to, send, recv):
        slot = src_z * NX + src_x
        return rcopy(g.at[slot], g.at[slot], send, recv, b, z * NX + to)

    def push(d):
        src = lax.rem(z + NZL - d, NZL)
        x_copy(src, x, right, x_send.at[0, src], x_recv.at[0, src]).start()
        x_copy(src, x, left, x_send.at[1, src], x_recv.at[1, src]).start()

    own.wait()
    push(0)
    for d in (1, 3, 2):
        zc[d - 1].wait_recv()
        push(d)
    for s in range(NZL // 2):
        t = s + NZL // 2
        x_copy(s, left, right, x_send.at[0, s], x_recv.at[0, s]).wait_recv()
        x_copy(s, left, right, r_send.at[0, s], r_recv.at[0, s]).start()
        x_copy(t, right, left, x_send.at[1, t], x_recv.at[1, t]).wait_recv()
        x_copy(t, right, left, r_send.at[1, s], r_recv.at[1, s]).start()
    for k in cots:
        k.wait_recv()
    own_cot.wait()
    for s in range(NZL // 2):
        t = s + NZL // 2
        x_copy(t, left, right, x_send.at[0, t], x_recv.at[0, t]).wait_recv()
        x_copy(s, right, left, x_send.at[1, s], x_recv.at[1, s]).wait_recv()
    for s in range(NZL // 2):
        x_copy(s, left, right, r_send.at[0, s], r_recv.at[0, s]).wait_recv()
        x_copy(s, left, right, r_send.at[1, s], r_recv.at[1, s]).wait_recv()

    feats = NZL * NX * fl
    mix = jnp.concatenate([w3v[s * NX + x] for s in range(NZL)], axis=0)
    wide = 256
    for n in range(quarter // wide):
        cut = slice(n * wide, (n + 1) * wide)
        pre = jnp.dot(mix, g[:, :, cut].reshape(feats, wide), preferred_element_type=F32)
        sig = jax.nn.sigmoid(pre)
        act[:, :, cut] = (pre * sig).astype(BF).reshape(NZL, fl, wide)
        grad_in = cotg[:, :, cut].reshape(NZL * fl, wide).astype(F32)
        pres[:, cut] = (grad_in * sig * (1.0 + pre * (1.0 - sig))).astype(BF)

    ac = [
        rcopy(act.at[zl(d)], part(act_out, z), a_send.at[d - 1], a_recv.at[d - 1], b, zl(d) * NX + x)
        for d in range(1, NZL)
    ]
    halves = NZL * NX // NC

    def grad_half(h):
        cols = g[pl.ds(h * halves, halves)].reshape(halves * fl, quarter)
        got = lax.dot_general(pres[...], cols, NT, preferred_element_type=F32)
        for s in range(NZL):
            for j in range(NY):
                rt, lt = divmod(j, 2)
                pt[h, j, s] = got[s * fl + rt * 8 : s * fl + (rt + 1) * 8, lt * TILE : (lt + 1) * TILE]

    grad_half(1 - core)
    pair = rcopy(pt.at[1 - core], sb, p_sem.at[0], p_sem.at[1], sib, c)
    pair.start()
    for k in ac:
        k.start()
    own_act = pltpu.make_async_copy(act.at[z], part(act_out, z), a_loc)
    own_act.start()
    grad_half(core)
    pair.wait_recv()
    qb[...] = pt[core] + sb[...]

    def y_copy(d):
        return rcopy(qb.at[y_peer(d)], yb.at[d], y_send.at[d], y_recv.at[d], y_blk(y_peer(d)), c)

    loop(1, NY, lambda d: y_copy(d).start())
    loop(1, NY, lambda d: y_copy(d).wait_recv())
    total = qb[y]
    for d in range(1, NY):
        total = total + yb[d]
    st[...] = total

    def q_copy(d):
        return rcopy(st.at[z_peer(d)[1]], zb.at[d], q_send.at[d], q_recv.at[d], *z_dev(*z_peer(d)))

    loop(1, NZ, lambda d: q_copy(d).start())
    loop(1, NZ, lambda d: q_copy(d).wait_recv())
    tile = st[z]
    for d in range(1, NZ):
        tile = tile + zb[d]
    wg_out[core, y] = tile

    def o_copy(d):
        return rcopy(wg_out.at[core, y], wg_out.at[core, y], o_send.at[d], o_recv.at[d], y_blk(y_peer(d)), c)

    loop(1, NY, lambda d: o_copy(d).start())
    loop(1, NY, lambda d: o_copy(d).wait_recv())
    last = rcopy(wg_out.at[core], wg_out.at[core], t_sem.at[0], t_sem.at[1], sib, c)
    last.start()

    loop(1, CHIPS, lambda d: hub_copy(d).wait_send())
    swap.wait_send()
    to_cross.wait_send()
    to_sib.wait_send()
    for k in cots + zc:
        k.wait_send()
    for s in range(NZL):
        x_copy(s, x, right, x_send.at[0, s], x_recv.at[0, s]).wait_send()
        x_copy(s, x, left, x_send.at[1, s], x_recv.at[1, s]).wait_send()
    for s in range(NZL // 2):
        x_copy(s, left, right, r_send.at[0, s], r_recv.at[0, s]).wait_send()
        x_copy(s, left, left, r_send.at[1, s], r_recv.at[1, s]).wait_send()
    pair.wait_send()
    for k in ac:
        k.wait_send()
    loop(1, NY, lambda d: y_copy(d).wait_send())
    loop(1, NZ, lambda d: q_copy(d).wait_send())
    loop(1, NY, lambda d: o_copy(d).wait_send())
    for k in ac:
        k.wait_recv()
    own_act.wait()
    last.wait()


DMA = pltpu.SemaphoreType.DMA


def body(
    features, band_weights, hub_ids, tile_rows, tile_cols, tile_vals, tile_counts, weight, cotangent
):
    fl, rows = features.shape
    blocks = rows // TILE
    quarter = rows // NZL
    slots = tile_vals.shape[0]
    cols = NZL * NX
    sds = jax.ShapeDtypeStruct
    act, wg = pl.pallas_call(
        layer_kernel,
        name="layer",
        out_shape=(sds((fl, rows), BF), sds((NC, NY, 8, TILE), F32)),
        in_specs=[SMEM] + [HBM] * 8,
        out_specs=(ANY, VMEM),
        scratch_shapes=[
            pltpu.VMEM((fl, rows + 2 * TILE), BF),
            pltpu.VMEM((rows, 3 * TILE), BF),
            pltpu.VMEM((1, hub_ids.shape[0]), jnp.int32),
            pltpu.VMEM((1, slots), jnp.int32),
            pltpu.SMEM((slots,), jnp.int32),
            pltpu.VMEM(tile_vals.shape, BF),
            pltpu.VMEM((NZL, fl, quarter), BF),
            pltpu.VMEM((cols, fl, weight.shape[1]), BF),
            pltpu.VMEM((blocks, fl, TILE), F32),
            pltpu.VMEM((2, CHIPS, fl // 2, TILE), BF),
            pltpu.VMEM((CHIPS, fl, TILE), BF),
            pltpu.VMEM((fl * slots, TILE), F32),
            pltpu.VMEM((blocks * fl, TILE), F32),
            pltpu.VMEM((NZL, fl, quarter), BF),
            pltpu.VMEM((cols, fl, quarter), BF),
            pltpu.VMEM((NZL, fl, quarter), BF),
            pltpu.VMEM((NZL * fl, quarter), BF),
            pltpu.VMEM((NC, NY, NZL, 8, TILE), F32),
            pltpu.VMEM((NY, NZL, 8, TILE), F32),
            pltpu.VMEM((NY, NZL, 8, TILE), F32),
            pltpu.VMEM((NY, NZL, 8, TILE), F32),
            pltpu.VMEM((NZL, 8, TILE), F32),
            pltpu.VMEM((NZ, 8, TILE), F32),
            DMA((8,)), DMA((CHIPS,)), DMA((CHIPS,)), DMA((2,)), DMA((2,)), DMA((2,)), DMA((3,)), DMA((3,)), DMA,
            DMA((3,)), DMA((3,)), DMA, DMA((2, NZL)), DMA((2, NZL)), DMA((2, 2)), DMA((2, 2)), DMA((3,)), DMA((3,)), DMA,
            DMA((2,)), DMA((NY,)), DMA((NY,)), DMA((NZ,)), DMA((NZ,)), DMA((NY,)), DMA((NY,)), DMA((2,)),
        ],
        compiler_params=pltpu.CompilerParams(
            collective_id=0, has_side_effects=True, vmem_limit_bytes=60 << 20
        ),
    )(
        tile_counts, features, band_weights, hub_ids.reshape(1, -1), tile_rows.reshape(1, -1), tile_cols,
        tile_vals, cotangent, weight.reshape(cols, fl, weight.shape[1]),
    )
    grad = wg.reshape(NC, 4, 2, 8, TILE).transpose(1, 3, 0, 2, 4).reshape(fl, 4 * TILE)
    return act, grad


def solution(mesh):
    in_specs = (
        P("col", "blk"),
        P("blk", None),
        P("blk"),
        P("blk"),
        P("blk"),
        P("blk", None, None),
        P("blk"),
        P(),
        P("col", "blk"),
    )
    out_specs = (P("col", "blk"), P("col", None))
    return jax.shard_map(body, mesh=mesh, in_specs=in_specs, out_specs=out_specs, check_vma=False)
```

time: 690 us -> 79.3 us (0.11)
  waiting for transfers between devices: 539 us -> 0 us
  blocking collectives: 81.8 us -> 0 us
  Pallas kernels: 0 us -> 74.7 us
  starting transfers between devices: 14.4 us -> 0 us
  matrix products: 14.1 us -> 0 us
  between operations: 14.8 us -> 1.29 us
  local copies, waits for them, and re-layouts: 16.2 us -> 3.14 us
  other arithmetic: 8.64 us -> 0 us
    psum x1 -> x0, waiting for transfers between devices: 461 us -> none  [body(): weight_grad = lax.psum(outer_rows(pre_grad, gathered), 'blk')]
    all_gather x1 -> x0, blocking collectives: 81.8 us -> none  [body(): all_hubs = lax.all_gather(own_hubs, 'blk', axis=1, tiled=True)]
    all_gather x1 -> x0, waiting for transfers between devices: 77.9 us -> none  [body(): gathered = lax.all_gather(aggregated, 'col', axis=0, tiled=True)]
    pallas_call x0 -> x1, Pallas kernels: none -> 74.7 us  [body(): pl.pallas_call(layer_kernel, name='layer', out_shape=(sds((fl, rows), BF)...]
    ppermute x2 -> x0, starting transfers between devices: 14.3 us -> none  [the longest x1 12 us: extended_2(): before = lax.ppermute(last, axis, up)]
    dot_general x4 -> x0, matrix products: 14.1 us -> none  [the longest x1 4.84 us: body(): jnp.einsum('ftj,trj->ftr', sources, tile_vals, preferred_element_type=jnp...]
    reshape x3 -> x0, local copies, waits for them, and re-layouts: 9.21 us -> none  [the longest x1 9.02 us: body(): band_blocks = band_weights.reshape(row_blocks, tile_size, 3, tile_size)]
  transfers between devices with their start and end apart: 4 -> 0, of which waited for: 2 -> 0; matrix products, arithmetic and copies ran while one was open for 3% -> 0% of each run, Pallas kernels for 0% -> 0%
where the time goes in v2:
time: 79.3 us; the launch traced here: 79.1 us
  Pallas kernels  74.7 us (94%)
  local copies, waits for them, and re-layouts  3.14 us (4%)
  between operations  1.29 us (2%)
    pallas_call x1, Pallas kernels, body(): pl.pallas_call(layer_kernel, name='layer', out_shape=(sds((fl, rows), BF)...  74.7 us
    unnamed x1, local copies, waits for them, and re-layouts  1.67 us

profile of v2, /device:TPU:1, one launch (start us, length us, event | category | flops | bytes accessed | tf_op | source)
XLA Modules:
  0.0 79.1 jit_solution(3056993345261618393)
XLA Ops:
  1.3 74.7 %layer.1 = (bf16[32,4096]{1,0:T(8,128)(2,1)}, f32[2,8,8,128]{3,2,1,0:T(8,128)}) custom-call(s32[1]{0:T(128)S(6)} %copy.13.count, bf16[32,4096]{1,0:T(8,128)(2,1)} %feat.1, bf16[4096,384]{1,0:T(8,128)(2,1)} %bw.1, s32[1,64]{1,0:T(1,128)} %bitcast.10, s32[1,128]{1,0:T(1,128)} %bitcast.11, s32[128]{0:T(128)} %col_ids.1, bf16[128,128,128]{2,1,0:T(8,128)(2,1)} %tv.1, ...), custom_call_target="tpu_custom_call" | custom-call | tf_op jit(solution)/shard_map/layer/pallas_call | solution.py:362
  76.0 1.5 %copy.11 = f32[4,8,2,2,128]{4,1,3,2,0:T(8,128)} copy(f32[4,8,2,2,128]{4,1,3,0,2:T(8,128)} %bitcast.9) | data formatting | bytes 131072 | tf_op jit(solution)/shard_map/transpose | solution.py:403
  77.5 1.7 %copy.14 = bf16[32,4096]{1,0:T(8,128)(2,1)} copy(bf16[32,4096]{1,0:T(8,128)(2,1)} %get-tuple-element.8) | data formatting | bytes 524288

commit v3 on v2

--- a/solution.py
+++ b/solution.py
@@ -36,6 +36,10 @@
     pl.semaphore_signal(sem, inc=1, device_id={"blk": blk, "col": col}, device_id_type=MESH)
 
 
+def far_first(count):
+    return sorted(range(1, count), key=lambda d: (-min(d, count - d), d))
+
+
 def loop(start, stop, body):
     lax.fori_loop(start, stop, lambda i, c: (body(i), c)[1], 0)
 
@@ -44,7 +48,7 @@
     count, feat, bw, ids, row_ids, col_ids, tv, cot, w3, act_out, wg_out,
     xe, wv, idv, rowv, colv, tvv, cotg, w3v, band, hubs, hub, part_s, hub_sum, aggq, g, act, pres, pt, sb, qb, yb, st, zb,
     in_sem, h_send, h_recv, s_sem, e_send, e_recv, c_send, c_recv, c_loc,
-    z_send, z_recv, z_loc, x_send, x_recv, r_send, r_recv, a_send, a_recv, a_loc,
+    z_send, z_recv, x_send, x_recv, r_send, r_recv, a_send, a_recv, a_loc,
     p_sem, y_send, y_recv, q_send, q_recv, o_send, o_recv, t_sem,
 ):
     rows = bw.shape[0]
@@ -86,18 +90,6 @@
     def z_dev(h, l):
         return (y * NZH + h) * NC + core, l * NX + x
 
-    barrier = pltpu.get_barrier_semaphore()
-    loop(1, CHIPS, lambda d: signal(barrier, hub_peer(d), c))
-    signal(barrier, cross, c)
-    for i in range(1, NZH):
-        for d in range(1, NZL):
-            signal(barrier, *z_dev(lax.rem(zh + i, NZH), zl(d)))
-    for d in range(1, NZL):
-        signal(barrier, b, zl(d) * NX + x)
-    signal(barrier, b, z * NX + left)
-    signal(barrier, b, z * NX + right)
-    signal(barrier, sib, c)
-
     loads = [
         pltpu.make_async_copy(src, dst, in_sem.at[i])
         for i, (src, dst) in enumerate(
@@ -113,7 +105,21 @@
             ]
         )
     ]
-    for k in loads:
+    loads[0].start()
+    loads[1].start()
+    barrier = pltpu.get_barrier_semaphore()
+    for d in far_first(CHIPS):
+        signal(barrier, hub_peer(d), c)
+    signal(barrier, cross, c)
+    for i in range(1, NZH):
+        for d in range(1, NZL):
+            signal(barrier, *z_dev(lax.rem(zh + i, NZH), zl(d)))
+    for d in range(1, NZL):
+        signal(barrier, b, zl(d) * NX + x)
+    signal(barrier, b, z * NX + left)
+    signal(barrier, b, z * NX + right)
+    signal(barrier, sib, c)
+    for k in loads[2:]:
         k.start()
 
     loads[0].wait()
@@ -135,7 +141,8 @@
     def hub_copy(d):
         return rcopy(hubs.at[0, chip], hubs.at[0, chip], h_send.at[d], h_recv.at[d], hub_peer(d), c)
 
-    loop(1, CHIPS, lambda d: hub_copy(d).start())
+    for d in far_first(CHIPS):
+        hub_copy(d).start()
     end = (blocks - 1) * TILE
     to_sib = rcopy(
         feat.at[:, pl.ds(pl.multiple_of((1 - core) * end, TILE), TILE)],
@@ -195,14 +202,16 @@
     hub[:, :half, :] = jnp.where(low3, first, pltpu.roll(second, TILE // 2, 2)).astype(BF)
     hub[:, half:, :] = jnp.where(low3, pltpu.roll(first, TILE // 2, 2), second).astype(BF)
 
-    def some_slots(i):
-        for j in range(8):
-            s = i * 8 + j
-            part_s[pl.ds(s, fl, stride=slots), :] = lax.dot_general(
-                hub[colv[s]], tvv[s], NT, preferred_element_type=F32
-            )
-
-    loop(0, slots // 8, some_slots)
+    def some_pairs(i):
+        for j in range(16):
+            s = (i * 16 + j) * 2
+            two = jnp.concatenate([hub[colv[s]], hub[colv[s + 1]]], axis=0)
+            tiles = tvv[pl.ds(s, 2)].reshape(2 * TILE, TILE)
+            got = lax.dot_general(two, tiles, NT, preferred_element_type=F32)
+            part_s[pl.ds(s, fl, stride=slots), :] = got[:fl, :TILE]
+            part_s[pl.ds(s + 1, fl, stride=slots), :] = got[fl:, TILE:]
+
+    loop(0, slots // 32, some_pairs)
     for f in range(fl):
         value = part_s[f * slots : (f + 1) * slots, :]
         high = value.astype(BF)
@@ -211,69 +220,94 @@
             place, jnp.concatenate([high, rest], axis=0), preferred_element_type=F32
         )
 
-    def round_part(q):
+    wide = quarter // 2
+
+    def side(ref, h):
+        return ref.at[:, pl.ds(h * wide, wide)]
+
+    def rounded(r):
+        at = pl.ds(pl.multiple_of(r * fl, fl), fl)
+        return (band[r] + hub_sum[at, :]).astype(BF)
+
+    def z_copy(d, h):
+        i = h * (NZL - 1) + d - 1
+        return rcopy(side(aggq.at[zl(d)], h), side(g.at[c], h), z_send.at[i], z_recv.at[i], b, zl(d) * NX + x)
+
+    def x_copy(src_z, src_x, h, to, way):
+        slot = side(g.at[src_z * NX + src_x], h)
+        return rcopy(slot, slot, x_send.at[way, h, src_z], x_recv.at[way, h, src_z], b, z * NX + to)
+
+    def relay(src_z, h):
+        origin, to = (left, right) if h == 0 else (right, left)
+        slot = side(g.at[src_z * NX + origin], h)
+        return rcopy(slot, slot, r_send.at[h, src_z], r_recv.at[h, src_z], b, z * NX + to)
+
+    def source(d):
+        return lax.rem(z + NZL - d, NZL)
+
+    def push(d, h):
+        x_copy(source(d), x, h, right, 0).start()
+        x_copy(source(d), x, h, left, 1).start()
+
+    def pass_on(d, h):
+        x_copy(source(d), x, h, right, h).wait_recv()
+        relay(source(d), h).start()
+
+    turns = (1, 3, 2)
+    for d in (2, 1, 3):
         for j in range(per):
-            r = q * per + j
-            at = pl.ds(pl.multiple_of(r * fl, fl), fl)
-            aggq[q, :, j * TILE : (j + 1) * TILE] = (band[r] + hub_sum[at, :]).astype(BF)
-
-    zc = [
-        rcopy(aggq.at[zl(d)], g.at[c], z_send.at[d - 1], z_recv.at[d - 1], b, zl(d) * NX + x)
-        for d in range(1, NZL)
-    ]
+            aggq[zl(d), :, j * TILE : (j + 1) * TILE] = rounded(zl(d) * per + j)
+        z_copy(d, 0).start()
+    for j in range(per):
+        g[c, :, j * TILE : (j + 1) * TILE] = rounded(z * per + j)
+    push(0, 0)
     for d in (2, 1, 3):
-        round_part(zl(d))
-        zc[d - 1].start()
-    round_part(z)
-    own = pltpu.make_async_copy(aggq.at[z], g.at[c], z_loc)
-    own.start()
-
-    def x_copy(src_z, src_x, to, send, recv):
-        slot = src_z * NX + src_x
-        return rcopy(g.at[slot], g.at[slot], send, recv, b, z * NX + to)
-
-    def push(d):
-        src = lax.rem(z + NZL - d, NZL)
-        x_copy(src, x, right, x_send.at[0, src], x_recv.at[0, src]).start()
-        x_copy(src, x, left, x_send.at[1, src], x_recv.at[1, src]).start()
-
-    own.wait()
-    push(0)
-    for d in (1, 3, 2):
-        zc[d - 1].wait_recv()
-        push(d)
-    for s in range(NZL // 2):
-        t = s + NZL // 2
-        x_copy(s, left, right, x_send.at[0, s], x_recv.at[0, s]).wait_recv()
-        x_copy(s, left, right, r_send.at[0, s], r_recv.at[0, s]).start()
-        x_copy(t, right, left, x_send.at[1, t], x_recv.at[1, t]).wait_recv()
-        x_copy(t, right, left, r_send.at[1, s], r_recv.at[1, s]).start()
+        z_copy(d, 1).start()
+    push(0, 1)
+    for n, d in enumerate(turns):
+        z_copy(d, 0).wait_recv()
+        push(d, 0)
+        if n == 0:
+            pass_on(0, 0)
+        if n == 1:
+            pass_on(0, 1)
+    for d in turns:
+        z_copy(d, 1).wait_recv()
+        push(d, 1)
+        pass_on(d, 0)
+    for d in turns:
+        pass_on(d, 1)
     for k in cots:
         k.wait_recv()
     own_cot.wait()
-    for s in range(NZL // 2):
-        t = s + NZL // 2
-        x_copy(t, left, right, x_send.at[0, t], x_recv.at[0, t]).wait_recv()
-        x_copy(s, right, left, x_send.at[1, s], x_recv.at[1, s]).wait_recv()
-    for s in range(NZL // 2):
-        x_copy(s, left, right, r_send.at[0, s], r_recv.at[0, s]).wait_recv()
-        x_copy(s, left, right, r_send.at[1, s], r_recv.at[1, s]).wait_recv()
 
     feats = NZL * NX * fl
     mix = jnp.concatenate([w3v[s * NX + x] for s in range(NZL)], axis=0)
-    wide = 256
-    for n in range(quarter // wide):
-        cut = slice(n * wide, (n + 1) * wide)
-        pre = jnp.dot(mix, g[:, :, cut].reshape(feats, wide), preferred_element_type=F32)
-        sig = jax.nn.sigmoid(pre)
-        act[:, :, cut] = (pre * sig).astype(BF).reshape(NZL, fl, wide)
-        grad_in = cotg[:, :, cut].reshape(NZL * fl, wide).astype(F32)
-        pres[:, cut] = (grad_in * sig * (1.0 + pre * (1.0 - sig))).astype(BF)
-
-    ac = [
-        rcopy(act.at[zl(d)], part(act_out, z), a_send.at[d - 1], a_recv.at[d - 1], b, zl(d) * NX + x)
-        for d in range(1, NZL)
-    ]
+
+    def a_copy(d, h):
+        i = h * (NZL - 1) + d - 1
+        return rcopy(side(act.at[zl(d)], h), side(part(act_out, z), h), a_send.at[i], a_recv.at[i], b, zl(d) * NX + x)
+
+    def own_act(h):
+        return pltpu.make_async_copy(side(act.at[z], h), side(part(act_out, z), h), a_loc.at[h])
+
+    step = 256
+    for h in range(2):
+        for d in range(NZL):
+            x_copy(source(d), x, h, right, 1 - h).wait_recv()
+            relay(source(d), h).wait_recv()
+        for n in range(h * wide // step, (h + 1) * wide // step):
+            cut = slice(n * step, (n + 1) * step)
+            pre = jnp.dot(mix, g[:, :, cut].reshape(feats, step), preferred_element_type=F32)
+            sig = jax.nn.sigmoid(pre)
+            act[:, :, cut] = (pre * sig).astype(BF).reshape(NZL, fl, step)
+            grad_in = cotg[:, :, cut].reshape(NZL * fl, step).astype(F32)
+            pres[:, cut] = (grad_in * sig * (1.0 + pre * (1.0 - sig))).astype(BF)
+        if h == 0:
+            for d in range(1, NZL):
+                a_copy(d, h).start()
+            own_act(h).start()
+
     halves = NZL * NX // NC
 
     def grad_half(h):
@@ -287,10 +321,9 @@
     grad_half(1 - core)
     pair = rcopy(pt.at[1 - core], sb, p_sem.at[0], p_sem.at[1], sib, c)
     pair.start()
-    for k in ac:
-        k.start()
-    own_act = pltpu.make_async_copy(act.at[z], part(act_out, z), a_loc)
-    own_act.start()
+    for d in range(1, NZL):
+        a_copy(d, 1).start()
+    own_act(1).start()
     grad_half(core)
     pair.wait_recv()
     qb[...] = pt[core] + sb[...]
@@ -298,7 +331,8 @@
     def y_copy(d):
         return rcopy(qb.at[y_peer(d)], yb.at[d], y_send.at[d], y_recv.at[d], y_blk(y_peer(d)), c)
 
-    loop(1, NY, lambda d: y_copy(d).start())
+    for d in far_first(NY):
+        y_copy(d).start()
     loop(1, NY, lambda d: y_copy(d).wait_recv())
     total = qb[y]
     for d in range(1, NY):
@@ -308,7 +342,8 @@
     def q_copy(d):
         return rcopy(st.at[z_peer(d)[1]], zb.at[d], q_send.at[d], q_recv.at[d], *z_dev(*z_peer(d)))
 
-    loop(1, NZ, lambda d: q_copy(d).start())
+    for d in far_first(NZ):
+        q_copy(d).start()
     loop(1, NZ, lambda d: q_copy(d).wait_recv())
     tile = st[z]
     for d in range(1, NZ):
@@ -318,7 +353,8 @@
     def o_copy(d):
         return rcopy(wg_out.at[core, y], wg_out.at[core, y], o_send.at[d], o_recv.at[d], y_blk(y_peer(d)), c)
 
-    loop(1, NY, lambda d: o_copy(d).start())
+    for d in far_first(NY):
+        o_copy(d).start()
     loop(1, NY, lambda d: o_copy(d).wait_recv())
     last = rcopy(wg_out.at[core], wg_out.at[core], t_sem.at[0], t_sem.at[1], sib, c)
     last.start()
@@ -327,23 +363,23 @@
     swap.wait_send()
     to_cross.wait_send()
     to_sib.wait_send()
-    for k in cots + zc:
+    for k in cots:
         k.wait_send()
-    for s in range(NZL):
-        x_copy(s, x, right, x_send.at[0, s], x_recv.at[0, s]).wait_send()
-        x_copy(s, x, left, x_send.at[1, s], x_recv.at[1, s]).wait_send()
-    for s in range(NZL // 2):
-        x_copy(s, left, right, r_send.at[0, s], r_recv.at[0, s]).wait_send()
-        x_copy(s, left, left, r_send.at[1, s], r_recv.at[1, s]).wait_send()
+    for h in range(2):
+        for d in range(1, NZL):
+            z_copy(d, h).wait_send()
+        for d in range(NZL):
+            x_copy(source(d), x, h, right, 0).wait_send()
+            x_copy(source(d), x, h, left, 1).wait_send()
+            relay(source(d), h).wait_send()
+        for d in range(1, NZL):
+            a_copy(d, h).wait_send()
+            a_copy(d, h).wait_recv()
+        own_act(h).wait()
     pair.wait_send()
-    for k in ac:
-        k.wait_send()
     loop(1, NY, lambda d: y_copy(d).wait_send())
     loop(1, NZ, lambda d: q_copy(d).wait_send())
     loop(1, NY, lambda d: o_copy(d).wait_send())
-    for k in ac:
-        k.wait_recv()
-    own_act.wait()
     last.wait()
 
 
@@ -390,7 +426,7 @@
             pltpu.VMEM((NZL, 8, TILE), F32),
             pltpu.VMEM((NZ, 8, TILE), F32),
             DMA((8,)), DMA((CHIPS,)), DMA((CHIPS,)), DMA((2,)), DMA((2,)), DMA((2,)), DMA((3,)), DMA((3,)), DMA,
-            DMA((3,)), DMA((3,)), DMA, DMA((2, NZL)), DMA((2, NZL)), DMA((2, 2)), DMA((2, 2)), DMA((3,)), DMA((3,)), DMA,
+            DMA((6,)), DMA((6,)), DMA((2, 2, NZL)), DMA((2, 2, NZL)), DMA((2, NZL)), DMA((2, NZL)), DMA((6,)), DMA((6,)), DMA((2,)),
             DMA((2,)), DMA((NY,)), DMA((NY,)), DMA((NZ,)), DMA((NZ,)), DMA((NY,)), DMA((NY,)), DMA((2,)),
         ],
         compiler_params=pltpu.CompilerParams(

time: 79.3 us -> 74.1 us (0.934)
  Pallas kernels: 74.7 us -> 69.5 us
    pallas_call x1, Pallas kernels: 74.7 us -> 69.5 us  [body(): pl.pallas_call(layer_kernel, name='layer', out_shape=(sds((fl, rows), BF)...]
where the time goes in v3:
time: 74.1 us; the launch traced here: 73.9 us
  Pallas kernels  69.5 us (94%)
  local copies, waits for them, and re-layouts  3.14 us (4%)
  between operations  1.29 us (2%)
    pallas_call x1, Pallas kernels, body(): pl.pallas_call(layer_kernel, name='layer', out_shape=(sds((fl, rows), BF)...  69.5 us
    unnamed x1, local copies, waits for them, and re-layouts  1.67 us

profile of v3, /device:TPU:1, one launch (start us, length us, event | category | flops | bytes accessed | tf_op | source)
XLA Modules:
  0.0 73.9 jit_solution(3115497659390558024)
XLA Ops:
  1.3 69.5 %layer.1 = (bf16[32,4096]{1,0:T(8,128)(2,1)}, f32[2,8,8,128]{3,2,1,0:T(8,128)}) custom-call(s32[1]{0:T(128)S(6)} %copy.13.count, bf16[32,4096]{1,0:T(8,128)(2,1)} %feat.1, bf16[4096,384]{1,0:T(8,128)(2,1)} %bw.1, s32[1,64]{1,0:T(1,128)} %bitcast.10, s32[1,128]{1,0:T(1,128)} %bitcast.11, s32[128]{0:T(128)} %col_ids.1, bf16[128,128,128]{2,1,0:T(8,128)(2,1)} %tv.1, ...), custom_call_target="tpu_custom_call" | custom-call | tf_op jit(solution)/shard_map/layer/pallas_call | solution.py:398
  70.8 1.5 %copy.11 = f32[4,8,2,2,128]{4,1,3,2,0:T(8,128)} copy(f32[4,8,2,2,128]{4,1,3,0,2:T(8,128)} %bitcast.9) | data formatting | bytes 131072 | tf_op jit(solution)/shard_map/transpose | solution.py:439
  72.2 1.7 %copy.14 = bf16[32,4096]{1,0:T(8,128)(2,1)} copy(bf16[32,4096]{1,0:T(8,128)(2,1)} %get-tuple-element.8) | data formatting | bytes 524288

commit v4 on v3

--- a/solution.py
+++ b/solution.py
@@ -40,13 +40,17 @@
     return sorted(range(1, count), key=lambda d: (-min(d, count - d), d))
 
 
+def near_first(count):
+    return far_first(count)[::-1]
+
+
 def loop(start, stop, body):
     lax.fori_loop(start, stop, lambda i, c: (body(i), c)[1], 0)
 
 
 def layer_kernel(
     count, feat, bw, ids, row_ids, col_ids, tv, cot, w3, act_out, wg_out,
-    xe, wv, idv, rowv, colv, tvv, cotg, w3v, band, hubs, hub, part_s, hub_sum, aggq, g, act, pres, pt, sb, qb, yb, st, zb,
+    xe, wv, idv, rowv, colv, tvv, cotg, w3v, band, hubs, hub, part_s, hub_sum, aggq, g, act, pres, grads, pt, sb, qb, yb, st, zb,
     in_sem, h_send, h_recv, s_sem, e_send, e_recv, c_send, c_recv, c_loc,
     z_send, z_recv, x_send, x_recv, r_send, r_recv, a_send, a_recv, a_loc,
     p_sem, y_send, y_recv, q_send, q_recv, o_send, o_recv, t_sem,
@@ -185,7 +189,8 @@
     place = jnp.where(same & used, 1.0, 0.0).astype(BF)
     place = jnp.concatenate([place, place], axis=1)
 
-    loop(1, CHIPS, lambda d: hub_copy(d).wait_recv())
+    for d in near_first(CHIPS):
+        hub_copy(d).wait_recv()
     swap = rcopy(hubs.at[0], hubs.at[1], s_sem.at[0], s_sem.at[1], sib, c)
     swap.start()
     to_cross.wait_recv()
@@ -203,15 +208,15 @@
     hub[:, half:, :] = jnp.where(low3, pltpu.roll(first, TILE // 2, 2), second).astype(BF)
 
     def some_pairs(i):
-        for j in range(16):
-            s = (i * 16 + j) * 2
+        for j in range(32):
+            s = (i * 32 + j) * 2
             two = jnp.concatenate([hub[colv[s]], hub[colv[s + 1]]], axis=0)
             tiles = tvv[pl.ds(s, 2)].reshape(2 * TILE, TILE)
             got = lax.dot_general(two, tiles, NT, preferred_element_type=F32)
             part_s[pl.ds(s, fl, stride=slots), :] = got[:fl, :TILE]
             part_s[pl.ds(s + 1, fl, stride=slots), :] = got[fl:, TILE:]
 
-    loop(0, slots // 32, some_pairs)
+    loop(0, slots // 64, some_pairs)
     for f in range(fl):
         value = part_s[f * slots : (f + 1) * slots, :]
         high = value.astype(BF)
@@ -291,6 +296,13 @@
     def own_act(h):
         return pltpu.make_async_copy(side(act.at[z], h), side(part(act_out, z), h), a_loc.at[h])
 
+    halves = NZL * NX // NC
+
+    def grad_part(k, h):
+        cut = slice(h * wide, (h + 1) * wide)
+        cols = g[pl.ds(k * halves, halves), :, cut].reshape(halves * fl, wide)
+        return lax.dot_general(pres[:, cut], cols, NT, preferred_element_type=F32)
+
     step = 256
     for h in range(2):
         for d in range(NZL):
@@ -307,16 +319,16 @@
             for d in range(1, NZL):
                 a_copy(d, h).start()
             own_act(h).start()
-
-    halves = NZL * NX // NC
-
-    def grad_half(h):
-        cols = g[pl.ds(h * halves, halves)].reshape(halves * fl, quarter)
-        got = lax.dot_general(pres[...], cols, NT, preferred_element_type=F32)
+            for k in range(NC):
+                grads[k] = grad_part(k, h)
+
+
+    def grad_half(k):
+        got = grads[k] + grad_part(k, 1)
         for s in range(NZL):
             for j in range(NY):
                 rt, lt = divmod(j, 2)
-                pt[h, j, s] = got[s * fl + rt * 8 : s * fl + (rt + 1) * 8, lt * TILE : (lt + 1) * TILE]
+                pt[k, j, s] = got[s * fl + rt * 8 : s * fl + (rt + 1) * 8, lt * TILE : (lt + 1) * TILE]
 
     grad_half(1 - core)
     pair = rcopy(pt.at[1 - core], sb, p_sem.at[0], p_sem.at[1], sib, c)
@@ -333,9 +345,9 @@
 
     for d in far_first(NY):
         y_copy(d).start()
-    loop(1, NY, lambda d: y_copy(d).wait_recv())
     total = qb[y]
-    for d in range(1, NY):
+    for d in near_first(NY):
+        y_copy(d).wait_recv()
         total = total + yb[d]
     st[...] = total
 
@@ -344,9 +356,9 @@
 
     for d in far_first(NZ):
         q_copy(d).start()
-    loop(1, NZ, lambda d: q_copy(d).wait_recv())
     tile = st[z]
-    for d in range(1, NZ):
+    for d in near_first(NZ):
+        q_copy(d).wait_recv()
         tile = tile + zb[d]
     wg_out[core, y] = tile
 
@@ -355,7 +367,8 @@
 
     for d in far_first(NY):
         o_copy(d).start()
-    loop(1, NY, lambda d: o_copy(d).wait_recv())
+    for d in near_first(NY):
+        o_copy(d).wait_recv()
     last = rcopy(wg_out.at[core], wg_out.at[core], t_sem.at[0], t_sem.at[1], sib, c)
     last.start()
 
@@ -381,6 +394,19 @@
     loop(1, NZ, lambda d: q_copy(d).wait_send())
     loop(1, NY, lambda d: o_copy(d).wait_send())
     last.wait()
+
+
+def write_kernel(act, tiles, act_out, grad_out, sem):
+    copies = [pltpu.make_async_copy(act, act_out, sem.at[NC * NY])]
+    for k in range(NC):
+        for j in range(NY):
+            rt, lt = divmod(j, 2)
+            to = grad_out.at[pl.ds(rt * 8, 8), pl.ds((k * 2 + lt) * TILE, TILE)]
+            copies.append(pltpu.make_async_copy(tiles.at[k, j], to, sem.at[k * NY + j]))
+    for k in copies:
+        k.start()
+    for k in copies:
+        k.wait()
 
 
 DMA = pltpu.SemaphoreType.DMA
@@ -419,6 +445,7 @@
             pltpu.VMEM((cols, fl, quarter), BF),
             pltpu.VMEM((NZL, fl, quarter), BF),
             pltpu.VMEM((NZL * fl, quarter), BF),
+            pltpu.VMEM((NC, NZL * fl, cols * fl // NC), F32),
             pltpu.VMEM((NC, NY, NZL, 8, TILE), F32),
             pltpu.VMEM((NY, NZL, 8, TILE), F32),
             pltpu.VMEM((NY, NZL, 8, TILE), F32),
@@ -430,14 +457,26 @@
             DMA((2,)), DMA((NY,)), DMA((NY,)), DMA((NZ,)), DMA((NZ,)), DMA((NY,)), DMA((NY,)), DMA((2,)),
         ],
         compiler_params=pltpu.CompilerParams(
-            collective_id=0, has_side_effects=True, vmem_limit_bytes=60 << 20
+            collective_id=0, has_side_effects=True, vmem_limit_bytes=40 << 20
         ),
     )(
-        tile_counts, features, band_weights, hub_ids.reshape(1, -1), tile_rows.reshape(1, -1), tile_cols,
-        tile_vals, cotangent, weight.reshape(cols, fl, weight.shape[1]),
+        tile_counts,
+        *(
+            pltpu.with_memory_space_constraint(k, pltpu.HBM)
+            for k in (
+                features, band_weights, hub_ids.reshape(1, -1), tile_rows.reshape(1, -1), tile_cols,
+                tile_vals, cotangent, weight.reshape(cols, fl, weight.shape[1]),
+            )
+        ),
     )
-    grad = wg.reshape(NC, 4, 2, 8, TILE).transpose(1, 3, 0, 2, 4).reshape(fl, 4 * TILE)
-    return act, grad
+    return pl.pallas_call(
+        write_kernel,
+        name="write",
+        out_shape=(sds((fl, rows), BF), sds((fl, NC * NY * 8 * TILE // fl), F32)),
+        in_specs=[VMEM, VMEM],
+        out_specs=(HBM, HBM),
+        scratch_shapes=[DMA((1 + NC * NY,))],
+    )(pltpu.with_memory_space_constraint(act, pltpu.VMEM), pltpu.with_memory_space_constraint(wg, pltpu.VMEM))
 
 
 def solution(mesh):

time: 74.1 us -> 71.1 us (0.960)
  local copies, waits for them, and re-layouts: 3.14 us -> 0 us
    unnamed x1 -> x0, local copies, waits for them, and re-layouts: 1.67 us -> none
    transpose x1 -> x0, local copies, waits for them, and re-layouts: 1.47 us -> none  [body(): wg.reshape(NC, 4, 2, 8, TILE).transpose(1, 3, 0, 2, 4).reshape(fl, 4 * TILE)]
    pallas_call x0 -> x1, Pallas kernels: none -> 0.89 us  [body(): pl.pallas_call(write_kernel, name='write', out_shape=(sds((fl, rows), BF)...]
where the time goes in v4:
time: 71.1 us; the launch traced here: 70.9 us
  Pallas kernels  69.6 us (98%)
  between operations  1.29 us (2%)
    pallas_call x1, Pallas kernels, body(): pl.pallas_call(layer_kernel, name='layer', out_shape=(sds((fl, rows), BF)...  68.8 us

profile of v4, /device:TPU:1, one launch (start us, length us, event | category | flops | bytes accessed | tf_op | source)
XLA Modules:
  0.0 70.9 jit_solution(15736044997825818673)
XLA Ops:
  1.3 68.8 %layer.1 = (bf16[32,4096]{1,0:T(8,128)(2,1)S(1)}, f32[2,8,8,128]{3,2,1,0:T(8,128)S(1)}) custom-call(s32[1]{0:T(128)S(6)} %copy.11.count, bf16[32,4096]{1,0:T(8,128)(2,1)} %feat.1, bf16[4096,384]{1,0:T(8,128)(2,1)} %bw.1, s32[1,64]{1,0:T(1,128)} %bitcast.4, s32[1,128]{1,0:T(1,128)} %bitcast.5, s32[128]{0:T(128)} %col_ids.1, bf16[128,128,128]{2,1,0:T(8,128)(2,1)} %tv.1, ...), custom_call_target="tpu_custom_call" | custom-call | tf_op jit(solution)/shard_map/layer/pallas_call | solution.py:424
  70.0 0.9 %write.1 = (bf16[32,4096]{1,0:T(8,128)(2,1)}, f32[32,512]{1,0:T(8,128)}) custom-call(bf16[32,4096]{1,0:T(8,128)(2,1)S(1)} %get-tuple-element.4.act, f32[2,8,8,128]{3,2,1,0:T(8,128)S(1)} %get-tuple-element.5.tiles), custom_call_target="tpu_custom_call" | custom-call | tf_op jit(solution)/shard_map/write/pallas_call | solution.py:472

commit v5 on v4

--- a/solution.py
+++ b/solution.py
@@ -21,6 +21,11 @@
 SMEM = pl.BlockSpec(memory_space=pltpu.SMEM)
 
 
+GRAD_STEPS = sorted(
+    [(d, k) for d in range(NY) for k in range(NC) if (d, k) != (0, 0)], key=lambda at: -min(at[0], NY - at[0])
+)
+
+
 def rcopy(src, dst, send, recv, blk, col):
     return pltpu.make_async_remote_copy(
         src_ref=src,
@@ -53,7 +58,7 @@
     xe, wv, idv, rowv, colv, tvv, cotg, w3v, band, hubs, hub, part_s, hub_sum, aggq, g, act, pres, grads, pt, sb, qb, yb, st, zb,
     in_sem, h_send, h_recv, s_sem, e_send, e_recv, c_send, c_recv, c_loc,
     z_send, z_recv, x_send, x_recv, r_send, r_recv, a_send, a_recv, a_loc,
-    p_sem, y_send, y_recv, q_send, q_recv, o_send, o_recv, t_sem,
+    p_sem, y_send, y_recv, q_send, q_recv, o_send, o_recv,
 ):
     rows = bw.shape[0]
     fl = feat.shape[0]
@@ -78,6 +83,9 @@
     def hub_peer(d):
         return lax.rem(chip + d, CHIPS) * NC + core
 
+    def y_dev(d, k):
+        return (lax.rem(y + d, NY) * NZH + zh) * NC + (core if k == 0 else 1 - core)
+
     def zl(d):
         return lax.rem(z + d, NZL)
 
@@ -114,6 +122,8 @@
     barrier = pltpu.get_barrier_semaphore()
     for d in far_first(CHIPS):
         signal(barrier, hub_peer(d), c)
+    for d in range(1, NY):
+        signal(barrier, y_dev(d, 1), c)
     signal(barrier, cross, c)
     for i in range(1, NZH):
         for d in range(1, NZL):
@@ -140,7 +150,7 @@
     low = lax.broadcasted_iota(jnp.int32, (half, TILE), 1) < TILE // 2
     hubs[0, chip] = jnp.where(low, picked[:half], picked[half:]).astype(BF)
 
-    pl.semaphore_wait(barrier, CHIPS - 1 + 1 + (NZH - 1) * (NZL - 1) + NZL - 1 + 2 + 1)
+    pl.semaphore_wait(barrier, CHIPS - 1 + NY - 1 + 1 + (NZH - 1) * (NZL - 1) + NZL - 1 + 2 + 1)
 
     def hub_copy(d):
         return rcopy(hubs.at[0, chip], hubs.at[0, chip], h_send.at[d], h_recv.at[d], hub_peer(d), c)
@@ -362,15 +372,14 @@
         tile = tile + zb[d]
     wg_out[core, y] = tile
 
-    def o_copy(d):
-        return rcopy(wg_out.at[core, y], wg_out.at[core, y], o_send.at[d], o_recv.at[d], y_blk(y_peer(d)), c)
-
-    for d in far_first(NY):
-        o_copy(d).start()
-    for d in near_first(NY):
-        o_copy(d).wait_recv()
-    last = rcopy(wg_out.at[core], wg_out.at[core], t_sem.at[0], t_sem.at[1], sib, c)
-    last.start()
+    def o_copy(d, k):
+        spot = wg_out.at[core, y]
+        return rcopy(spot, spot, o_send.at[k, d], o_recv.at[k, d], y_dev(d, k), c)
+
+    for at in GRAD_STEPS:
+        o_copy(*at).start()
+    for at in GRAD_STEPS[::-1]:
+        o_copy(*at).wait_recv()
 
     loop(1, CHIPS, lambda d: hub_copy(d).wait_send())
     swap.wait_send()
@@ -392,8 +401,8 @@
     pair.wait_send()
     loop(1, NY, lambda d: y_copy(d).wait_send())
     loop(1, NZ, lambda d: q_copy(d).wait_send())
-    loop(1, NY, lambda d: o_copy(d).wait_send())
-    last.wait()
+    for at in GRAD_STEPS:
+        o_copy(*at).wait_send()
 
 
 def write_kernel(act, tiles, act_out, grad_out, sem):
@@ -454,7 +463,7 @@
             pltpu.VMEM((NZ, 8, TILE), F32),
             DMA((8,)), DMA((CHIPS,)), DMA((CHIPS,)), DMA((2,)), DMA((2,)), DMA((2,)), DMA((3,)), DMA((3,)), DMA,
             DMA((6,)), DMA((6,)), DMA((2, 2, NZL)), DMA((2, 2, NZL)), DMA((2, NZL)), DMA((2, NZL)), DMA((6,)), DMA((6,)), DMA((2,)),
-            DMA((2,)), DMA((NY,)), DMA((NY,)), DMA((NZ,)), DMA((NZ,)), DMA((NY,)), DMA((NY,)), DMA((2,)),
+            DMA((2,)), DMA((NY,)), DMA((NY,)), DMA((NZ,)), DMA((NZ,)), DMA((NC, NY)), DMA((NC, NY)),
         ],
         compiler_params=pltpu.CompilerParams(
             collective_id=0, has_side_effects=True, vmem_limit_bytes=40 << 20

time: 71.1 us -> 69.7 us (0.980)
  Pallas kernels: 69.6 us -> 68.3 us
    pallas_call x1, Pallas kernels: 68.8 us -> 67.4 us  [body(): pl.pallas_call(layer_kernel, name='layer', out_shape=(sds((fl, rows), BF)...]
where the time goes in v5:
time: 69.7 us; the launch traced here: 69.6 us
  Pallas kernels  68.3 us (98%)
  between operations  1.29 us (2%)
    pallas_call x1, Pallas kernels, body(): pl.pallas_call(layer_kernel, name='layer', out_shape=(sds((fl, rows), BF)...  67.4 us

profile of v5, /device:TPU:1, one launch (start us, length us, event | category | flops | bytes accessed | tf_op | source)
XLA Modules:
  0.0 69.6 jit_solution(3394909002655945683)
XLA Ops:
  1.3 67.4 %layer.1 = (bf16[32,4096]{1,0:T(8,128)(2,1)S(1)}, f32[2,8,8,128]{3,2,1,0:T(8,128)S(1)}) custom-call(s32[1]{0:T(128)S(6)} %copy.11.count, bf16[32,4096]{1,0:T(8,128)(2,1)} %feat.1, bf16[4096,384]{1,0:T(8,128)(2,1)} %bw.1, s32[1,64]{1,0:T(1,128)} %bitcast.4, s32[1,128]{1,0:T(1,128)} %bitcast.5, s32[128]{0:T(128)} %col_ids.1, bf16[128,128,128]{2,1,0:T(8,128)(2,1)} %tv.1, ...), custom_call_target="tpu_custom_call" | custom-call | tf_op jit(solution)/shard_map/layer/pallas_call | solution.py:433
  68.7 0.9 %write.1 = (bf16[32,4096]{1,0:T(8,128)(2,1)}, f32[32,512]{1,0:T(8,128)}) custom-call(bf16[32,4096]{1,0:T(8,128)(2,1)S(1)} %get-tuple-element.4.act, f32[2,8,8,128]{3,2,1,0:T(8,128)S(1)} %get-tuple-element.5.tiles), custom_call_target="tpu_custom_call" | custom-call | tf_op jit(solution)/shard_map/write/pallas_call | solution.py:481

commit v6 on v5

--- a/solution.py
+++ b/solution.py
@@ -178,10 +178,7 @@
         rcopy(part(cot, zl(d)), cotg.at[z], c_send.at[d - 1], c_recv.at[d - 1], b, zl(d) * NX + x)
         for d in range(1, NZL)
     ]
-    for k in cots:
-        k.start()
     own_cot = pltpu.make_async_copy(part(cot, z), cotg.at[z], c_loc)
-    own_cot.start()
 
     def do_band(r):
         band[r] = lax.dot_general(
@@ -203,6 +200,9 @@
         hub_copy(d).wait_recv()
     swap = rcopy(hubs.at[0], hubs.at[1], s_sem.at[0], s_sem.at[1], sib, c)
     swap.start()
+    for k in cots:
+        k.start()
+    own_cot.start()
     to_cross.wait_recv()
     to_sib.wait_recv()
     do_band(0)

time: 69.7 us -> 71.4 us (1.024)
  Pallas kernels: 68.3 us -> 69.4 us
    pallas_call x1, Pallas kernels: 67.4 us -> 68.5 us  [body(): pl.pallas_call(layer_kernel, name='layer', out_shape=(sds((fl, rows), BF)...]
where the time goes in v6:
time: 71.4 us; the launch traced here: 70.7 us
  Pallas kernels  69.4 us (97%)
  between operations  1.29 us (2%)
    pallas_call x1, Pallas kernels, body(): pl.pallas_call(layer_kernel, name='layer', out_shape=(sds((fl, rows), BF)...  68.5 us

profile of v6, /device:TPU:1, one launch (start us, length us, event | category | flops | bytes accessed | tf_op | source)
XLA Modules:
  0.0 70.7 jit_solution(1259264572660823166)
XLA Ops:
  1.3 68.5 %layer.1 = (bf16[32,4096]{1,0:T(8,128)(2,1)S(1)}, f32[2,8,8,128]{3,2,1,0:T(8,128)S(1)}) custom-call(s32[1]{0:T(128)S(6)} %copy.11.count, bf16[32,4096]{1,0:T(8,128)(2,1)} %feat.1, bf16[4096,384]{1,0:T(8,128)(2,1)} %bw.1, s32[1,64]{1,0:T(1,128)} %bitcast.4, s32[1,128]{1,0:T(1,128)} %bitcast.5, s32[128]{0:T(128)} %col_ids.1, bf16[128,128,128]{2,1,0:T(8,128)(2,1)} %tv.1, ...), custom_call_target="tpu_custom_call" | custom-call | tf_op jit(solution)/shard_map/layer/pallas_call | solution.py:433
  69.8 0.9 %write.1 = (bf16[32,4096]{1,0:T(8,128)(2,1)}, f32[32,512]{1,0:T(8,128)}) custom-call(bf16[32,4096]{1,0:T(8,128)(2,1)S(1)} %get-tuple-element.4.act, f32[2,8,8,128]{3,2,1,0:T(8,128)S(1)} %get-tuple-element.5.tiles), custom_call_target="tpu_custom_call" | custom-call | tf_op jit(solution)/shard_map/write/pallas_call | solution.py:481
